TPU v7x, 32 devices: a whole 2x2x4 slice. The times are simulated.
32 devices in a mesh: dp: 8 (over z, y), tensor: 4 (over x, core).
Axes of the slice: x: 2, y: 2, z: 4, core: 2. Of those that a mesh axis runs over, the one named last changes fastest.
Arguments:
- tokens: bfloat16 [8192, 1536], P('dp', 'tensor'), may hold values from -6 to 6
- segments: int32 [8, 1024], P('dp'), may hold values from 0 to 7, never falling along the last dimension, each value on 1 to 512 neighbouring positions
- attn_gain: bfloat16 [1536], P('tensor'), may hold values from 0.25 to 1.75
- w_qkv: bfloat16 [3, 1536, 1536], P(None, None, 'tensor'), may hold values from -0.15625 to 0.15625
- kq_kernel: float32 [16, 6, 11], P('tensor'), may hold values from -0.8 to 1.8
- head_mix: float32 [16, 2], P('tensor'), may hold values from -0.6 to 1.3
- group_gain: bfloat16 [1536], P('tensor'), may hold values from 0.25 to 1.75
- w_out: bfloat16 [1536, 1536], P('tensor'), may hold values from -0.15625 to 0.15625
- mlp_gain: bfloat16 [1536], P('tensor'), may hold values from 0.25 to 1.75
- w_gate_up: bfloat16 [2, 1536, 4096], P(None, None, 'tensor'), may hold values from -0.15625 to 0.15625
- w_down: bfloat16 [4096, 1536], P('tensor'), may hold values from -0.09375 to 0.09375
- cotangent: bfloat16 [8192, 1536], P('dp', 'tensor'), may hold values from -6 to 6
Outputs:
- layer_out: bfloat16 [8192, 1536], P('dp', 'tensor')
- tokens_grad: float32 [8192, 1536], P('dp', 'tensor')
- attn_gain_grad: float32 [1536], P('tensor')
- w_qkv_grad: float32 [3, 1536, 1536], P(None, None, 'tensor')
- kq_kernel_grad: float32 [16, 6, 11], P('tensor')
- head_mix_grad: float32 [16, 2], P('tensor')
- group_gain_grad: float32 [1536], P('tensor')
- w_out_grad: float32 [1536, 1536], P('tensor')
- mlp_gain_grad: float32 [1536], P('tensor')
- w_gate_up_grad: float32 [2, 1536, 4096], P(None, None, 'tensor')
- w_down_grad: float32 [4096, 1536], P('tensor')
Inputs may be any that keep to these rules, and one draw needn't show every extreme that they name: `segments`: within a sequence the numbers never fall; each document holds at most 512 tokens.
All inputs are finite; a program needn't handle non-finite values.
Results may differ from a plain program's by a relative error of at most 0.018.
The roundings to bfloat16 on the way count: a program that leaves them out, or rounds other values in their place, can miss the bound.
Values may be sent and summed in bfloat16 or wider, within the bound.
A program may use at most 320 MiB of HBM per device.

v0:
```python
import functools

import jax
import jax.numpy as jnp
from jax import lax
from jax.experimental import pallas as pl
from jax.experimental.pallas import tpu as pltpu
from jax.sharding import PartitionSpec as P

HEAD_DIM = 96
PAD_DIM = 128
DOC_MOST = 512
EPS = 1e-05
NEG = -1e30

COST = pl.CostEstimate(flops=1 << 20, bytes_accessed=1 << 10, transcendentals=0)
EARLY_SHARE = 0.75
ROWS = 128
HALO = 16
WIN = 256
OWN = 16
STEP = WIN - 2 * OWN
TOP = 256
EXT = ROWS + HALO

F32 = jnp.float32
BF16 = jnp.bfloat16


def windows_most(key_half):
    return -(-(DOC_MOST - 1 + ROWS + key_half) // STEP)


def dot_nt(a, b):
    return lax.dot_general(a, b, (((1,), (1,)), ((), ())), preferred_element_type=F32)


def dot_tn(a, b):
    return lax.dot_general(a, b, (((0,), (0,)), ((), ())), preferred_element_type=F32)


def dot_nn(a, b):
    return jnp.dot(a, b, preferred_element_type=F32)


def fill_padded(dst, src, top, length):
    total = dst.shape[0]
    dst[0:top, :] = jnp.zeros((top, dst.shape[1]), dst.dtype)
    dst[top : top + length, :] = src[...]
    if total > top + length:
        dst[top + length : total, :] = jnp.zeros((total - top - length, dst.shape[1]), dst.dtype)


def lanes_between(first, last, width):
    lane = lax.broadcasted_iota(jnp.int32, (first.shape[0], width), 1)
    return (lane >= first) & (lane <= last)


def row_numbers(base, count):
    return base + lax.broadcasted_iota(jnp.int32, (count, 1), 0)


def forward_kernel(
    n_taps, key_half, most, count_ref, mix_ref, q_ref, k_ref, v_ref, start_ref, base_ref, gain_ref,
    probs_ref, heads_ref, grouped_ref, qs, ks, vs, logit_ref, band_ref, inputs,
):
    pair = pl.program_id(0)
    block = pl.program_id(1)
    length = q_ref.shape[0]
    scale = HEAD_DIM ** (-0.5)

    @pl.when(block == 0)
    def _():
        fill_padded(qs, q_ref, HALO, length)
        fill_padded(ks, k_ref, TOP, length)
        fill_padded(vs, v_ref, TOP, length)
        for s in range(2):
            for a in range(n_taps):
                band = banded(base_ref[s, a : a + 1, :])
                high = band.astype(BF16)
                band_ref[s, a, 0:WIN] = high
                band_ref[s, a, WIN : 2 * WIN] = high
                band_ref[s, a, 2 * WIN : 3 * WIN] = (band - high.astype(F32)).astype(BF16)

    row0 = pl.multiple_of(block * ROWS, ROWS)

    def body(n):
        start = start_ref[pl.ds(row0, EXT), :]
        place = row_numbers(row0 - HALO, EXT)
        firsts, lasts = [], []
        for k in range(n):
            base = row0 + ROWS - STEP * (k + 1) - OWN
            at = pl.multiple_of(TOP + base, 16)
            firsts.append(start - base)
            lasts.append(place - base)
            valid = lanes_between(firsts[k], lasts[k], WIN)
            rows = slice(k * EXT, (k + 1) * EXT)
            for s in range(2):
                cols = pl.ds(s * PAD_DIM, PAD_DIM)
                raw = dot_nt(qs[pl.ds(row0, EXT), cols], ks[pl.ds(at, WIN), cols])
                masked = jnp.where(valid, raw * scale, 0.0)
                high = masked.astype(BF16)
                inputs[s, rows, 0:WIN] = high
                inputs[s, rows, WIN : 2 * WIN] = (masked - high.astype(F32)).astype(BF16)
                inputs[s, rows, 2 * WIN : 3 * WIN] = high
        peaks = [None, None]
        for s in range(2):
            total = None
            for a in reversed(range(n_taps)):
                term = dot_nn(inputs[s, 0 : n * EXT, :], band_ref[s, a])
                total = term if total is None else pltpu.roll(total, 1, 0) + term
            for k in range(n):
                shown = lanes_between(
                    jnp.maximum(firsts[k][HALO:], key_half + 1),
                    jnp.minimum(lasts[k][HALO:], WIN - 2 - key_half),
                    WIN,
                )
                logits = jnp.where(shown, total[k * EXT + HALO : (k + 1) * EXT], NEG)
                logit_ref[s, k] = logits
                top = jnp.max(logits, axis=-1, keepdims=True)
                peaks[s] = top if peaks[s] is None else jnp.maximum(peaks[s], top)
        lane = lax.broadcasted_iota(jnp.int32, (ROWS, WIN), 1)
        own = (lane >= OWN) & (lane < WIN - OWN)
        sums = [None, None]
        for k in range(n):
            for s in range(2):
                expo = jnp.exp(logit_ref[s, k] - peaks[s])
                logit_ref[s, k] = expo
                part = jnp.sum(jnp.where(own, expo, 0.0), axis=-1, keepdims=True)
                sums[s] = part if sums[s] is None else sums[s] + part
        inverse = [1.0 / sums[s] for s in range(2)]
        outs = [None, None]
        for k in range(n):
            base = row0 + ROWS - STEP * (k + 1) - OWN
            at = pl.multiple_of(TOP + base, 16)
            probs = []
            for s in range(2):
                prob = logit_ref[s, k] * inverse[s]
                probs_ref[s, 0, k] = prob
                probs.append(jnp.where(own, prob, 0.0))
            for h in range(2):
                mixed = (
                    mix_ref[2 * pair + h, 0] * probs[0] + mix_ref[2 * pair + h, 1] * probs[1]
                ).astype(BF16)
                part = dot_nn(mixed, vs[pl.ds(at, WIN), pl.ds(h * PAD_DIM, PAD_DIM)])
                outs[h] = part if outs[h] is None else outs[h] + part
        for h in range(2):
            cols = slice(h * PAD_DIM, (h + 1) * PAD_DIM)
            out = outs[h]
            heads_ref[:, cols] = out
            factor = lax.rsqrt(jnp.sum(out * out, axis=-1, keepdims=True) * (1.0 / HEAD_DIM) + EPS)
            grouped_ref[:, cols] = (out * factor * gain_ref[:, cols]).astype(BF16)

    for n in range(1, most + 1):
        pl.when(count_ref[block] == n)(functools.partial(body, n))


def attend_forward(proj, start, counts, base, mix, gain):
    length = proj.shape[0]
    heads, n_taps = base.shape[:2]
    pairs = heads // 2
    blocks = length // ROWS
    key_half = 5
    most = windows_most(key_half)
    two = 2 * PAD_DIM
    grid_spec = pltpu.PrefetchScalarGridSpec(
        num_scalar_prefetch=2,
        grid=(pairs, blocks),
        in_specs=[
            pl.BlockSpec((length, two), lambda p, b, *_: (0, p)),
            pl.BlockSpec((length, two), lambda p, b, *_: (0, pairs + p)),
            pl.BlockSpec((length, two), lambda p, b, *_: (0, 2 * pairs + p)),
            pl.BlockSpec((HALO + length, 1), lambda p, b, *_: (0, 0)),
            pl.BlockSpec((2, n_taps, WIN), lambda p, b, *_: (p, 0, 0)),
            pl.BlockSpec((1, two), lambda p, b, *_: (0, p)),
        ],
        out_specs=[
            pl.BlockSpec((2, 1, most, ROWS, WIN), lambda p, b, *_: (p, b, 0, 0, 0)),
            pl.BlockSpec((ROWS, two), lambda p, b, *_: (b, p)),
            pl.BlockSpec((ROWS, two), lambda p, b, *_: (b, p)),
        ],
        scratch_shapes=[
            pltpu.VMEM((HALO + length, two), BF16),
            pltpu.VMEM((TOP + length + HALO, two), BF16),
            pltpu.VMEM((TOP + length + HALO, two), BF16),
            pltpu.VMEM((2, most, ROWS, WIN), F32),
            pltpu.VMEM((2, n_taps, 3 * WIN, WIN), BF16),
            pltpu.VMEM((2, most * EXT, 3 * WIN), BF16),
        ],
    )
    return pl.pallas_call(
        functools.partial(forward_kernel, n_taps, key_half, most),
        grid_spec=grid_spec,
        out_shape=[
            jax.ShapeDtypeStruct((heads, blocks, most, ROWS, WIN), F32),
            jax.ShapeDtypeStruct((length, heads * PAD_DIM), F32),
            jax.ShapeDtypeStruct((length, heads * PAD_DIM), BF16),
        ],
        compiler_params=pltpu.CompilerParams(vmem_limit_bytes=56 << 20),
        cost_estimate=COST,
        name="attend_forward",
    )(counts, mix, proj, proj, proj, start, base, gain)


def backward_kernel(
    n_taps, key_half, most, count_ref, mix_ref, q_ref, k_ref, v_ref, start_ref, base_ref, gain_ref,
    probs_ref, heads_ref, grad_ref, dqkv_ref, inner_ref, gain_grad_ref, tap_ref, mix_grad_ref,
    qs, ks, vs, dq_sum, dk_sum, dv_sum, taps, inputs, tap_sum, mixed_grad, t_back_ref, kept, inner_sum,
):
    pair = pl.program_id(0)
    block = pl.program_id(1)
    length = q_ref.shape[0]
    scale = HEAD_DIM ** (-0.5)

    @pl.when(block == 0)
    def _():
        fill_padded(qs, q_ref, HALO, length)
        fill_padded(ks, k_ref, TOP, length)
        fill_padded(vs, v_ref, TOP, length)
        dq_sum[...] = jnp.zeros_like(dq_sum)
        dk_sum[...] = jnp.zeros_like(dk_sum)
        dv_sum[...] = jnp.zeros_like(dv_sum)
        tap_sum[...] = jnp.zeros_like(tap_sum)
        gain_grad_ref[...] = jnp.zeros_like(gain_grad_ref)
        mix_grad_ref[...] = jnp.zeros_like(mix_grad_ref)
        for s in range(2):
            for a in range(n_taps):
                t_back_ref[s, a * WIN : (a + 1) * WIN, :] = banded(base_ref[s, a : a + 1, :]).astype(BF16)

    row0 = pl.multiple_of(block * ROWS, ROWS)

    def body(n):
        grads = []
        for h in range(2):
            cols = slice(h * PAD_DIM, (h + 1) * PAD_DIM)
            out = heads_ref[:, cols]
            factor = lax.rsqrt(jnp.sum(out * out, axis=-1, keepdims=True) * (1.0 / HEAD_DIM) + EPS)
            unit = out * factor
            grad = grad_ref[:, cols]
            gain_grad_ref[:, cols] += jnp.sum(grad * unit, axis=0, keepdims=True)
            scaled = grad * gain_ref[:, cols]
            inner = jnp.sum(scaled * unit, axis=-1, keepdims=True) * (1.0 / HEAD_DIM)
            grads.append((factor * (scaled - unit * inner)).astype(BF16))
        lane = lax.broadcasted_iota(jnp.int32, (ROWS, WIN), 1)
        own = (lane >= OWN) & (lane < WIN - OWN)
        inner = [[None, None], [None, None]]
        for k in range(n):
            base = row0 + ROWS - STEP * (k + 1) - OWN
            at = pl.multiple_of(TOP + base, 16)
            probs = [jnp.where(own, probs_ref[s, 0, k], 0.0) for s in range(2)]
            for h in range(2):
                cols = pl.ds(h * PAD_DIM, PAD_DIM)
                grad_mixed = dot_nt(grads[h], vs[pl.ds(at, WIN), cols])
                mixed_grad[h, k] = grad_mixed
                for s in range(2):
                    part = jnp.sum(grad_mixed * probs[s], axis=-1, keepdims=True)
                    inner[h][s] = part if inner[h][s] is None else inner[h][s] + part
                mixed = (
                    mix_ref[2 * pair + h, 0] * probs[0] + mix_ref[2 * pair + h, 1] * probs[1]
                ).astype(BF16)
                dv_sum[pl.ds(at, WIN), cols] += dot_tn(mixed, grads[h])
        for h in range(2):
            for s in range(2):
                row = 2 * h + s
                mix_grad_ref[0, row : row + 1, :] += jnp.broadcast_to(
                    jnp.sum(inner[h][s], axis=0, keepdims=True), (1, PAD_DIM)
                )
        start = start_ref[pl.ds(row0, EXT), :]
        place = row_numbers(row0 - HALO, EXT)
        for s in range(2):
            cols = pl.ds(s * PAD_DIM, PAD_DIM)
            mix0 = mix_ref[2 * pair, s]
            mix1 = mix_ref[2 * pair + 1, s]
            delta = mix0 * inner[0][s] + mix1 * inner[1][s]
            query = qs[pl.ds(row0, EXT), cols]
            for k in range(n):
                grad_prob = mix0 * mixed_grad[0, k] + mix1 * mixed_grad[1, k]
                grad_logit = probs_ref[s, 0, k] * (grad_prob - delta)
                grown = jnp.concatenate([jnp.zeros((HALO, WIN), F32), grad_logit], axis=0)
                for a in range(n_taps):
                    moved = grown if a == 0 else pltpu.roll(grown, EXT - a, 0)
                    taps[k * EXT : (k + 1) * EXT, a * WIN : (a + 1) * WIN] = moved.astype(BF16)
            grad_inputs = dot_nn(taps[0 : n * EXT, :], t_back_ref[s])
            for k in range(n):
                base = row0 + ROWS - STEP * (k + 1) - OWN
                at = pl.multiple_of(TOP + base, 16)
                keys = ks[pl.ds(at, WIN), cols]
                mine = lanes_between(
                    jnp.maximum(start - base, OWN), jnp.minimum(place - base, WIN - OWN - 1), WIN
                )
                grad_masked = grad_inputs[k * EXT : (k + 1) * EXT]
                grad_score = jnp.where(mine, grad_masked * scale, 0.0).astype(BF16)
                dq_sum[pl.ds(row0, EXT), cols] += dot_nn(grad_score, keys)
                dk_sum[pl.ds(at, WIN), cols] += dot_tn(grad_score, query)
                raw = dot_nt(query, keys)
                inputs[k * EXT : (k + 1) * EXT, :] = jnp.where(mine, raw * scale, 0.0).astype(BF16)
            tap_sum[s] += dot_tn(inputs[0 : n * EXT, :], taps[0 : n * EXT, :])

    for n in range(1, most + 1):
        pl.when(count_ref[block] == n)(functools.partial(body, n))

    @pl.when(block == pl.num_programs(1) - 1)
    def _():
        inner = None
        sums = ((dq_sum, HALO, q_ref), (dk_sum, TOP, k_ref), (dv_sum, TOP, v_ref))
        for c, (total, top, given) in enumerate(sums):
            grad = total[top : top + length, :].astype(BF16)
            kept[pair, c] = grad
            part = jnp.sum(grad.astype(F32) * given[...].astype(F32), axis=-1, keepdims=True)
            inner = part if inner is None else inner + part

        @pl.when(pair == 0)
        def _():
            inner_sum[...] = inner

        @pl.when(pair > 0)
        def _():
            inner_sum[...] += inner

        row = lax.broadcasted_iota(jnp.int32, (WIN, WIN), 0)
        lane = lax.broadcasted_iota(jnp.int32, (WIN, WIN), 1)
        for s in range(2):
            for a in range(n_taps):
                whole = tap_sum[s, :, a * WIN : (a + 1) * WIN]
                for b in range(2 * key_half + 1):
                    part = jnp.where(lane - row == b - key_half, whole, 0.0)
                    part = jnp.sum(part, axis=0, keepdims=True)
                    part = jnp.sum(part, axis=1, keepdims=True)
                    at = a * (2 * key_half + 1) + b
                    tap_ref[s, at : at + 1, :] = jnp.broadcast_to(part, (1, PAD_DIM))

    pairs = kept.shape[0]

    @pl.when((block == pl.num_programs(1) - 1) & (pair == pairs - 1))
    def _():
        width = 2 * pairs * HEAD_DIM

        def rows_out(n, carry):
            at = pl.ds(pl.multiple_of(n * ROWS, ROWS), ROWS)
            for c in range(3):
                heads = [
                    kept[p, c, at, s * PAD_DIM : s * PAD_DIM + HEAD_DIM]
                    for p in range(pairs)
                    for s in range(2)
                ]
                dqkv_ref[at, c * width : (c + 1) * width] = jnp.concatenate(heads, axis=1)
            column = jnp.broadcast_to(inner_sum[at, :], (ROWS, PAD_DIM))
            inner_ref[pl.ds(n, 1), :] = column.T[0:1, :]
            return carry

        lax.fori_loop(0, length // ROWS, rows_out, 0)


def attend_backward(proj, start, counts, base, mix, gain, probs, heads_out, grad_grouped):
    length = proj.shape[0]
    heads, n_taps = base.shape[:2]
    pairs = heads // 2
    blocks = length // ROWS
    key_half = 5
    most = windows_most(key_half)
    two = 2 * PAD_DIM
    tap_rows = n_taps * (2 * key_half + 1)
    grid_spec = pltpu.PrefetchScalarGridSpec(
        num_scalar_prefetch=2,
        grid=(pairs, blocks),
        in_specs=[
            pl.BlockSpec((length, two), lambda p, b, *_: (0, p)),
            pl.BlockSpec((length, two), lambda p, b, *_: (0, pairs + p)),
            pl.BlockSpec((length, two), lambda p, b, *_: (0, 2 * pairs + p)),
            pl.BlockSpec((HALO + length, 1), lambda p, b, *_: (0, 0)),
            pl.BlockSpec((2, n_taps, WIN), lambda p, b, *_: (p, 0, 0)),
            pl.BlockSpec((1, two), lambda p, b, *_: (0, p)),
            pl.BlockSpec((2, 1, most, ROWS, WIN), lambda p, b, *_: (p, b, 0, 0, 0)),
            pl.BlockSpec((ROWS, two), lambda p, b, *_: (b, p)),
            pl.BlockSpec((ROWS, two), lambda p, b, *_: (b, p)),
        ],
        out_specs=[
            pl.BlockSpec((length, 3 * heads * HEAD_DIM), lambda p, b, *_: (0, 0)),
            pl.BlockSpec((length // ROWS, ROWS), lambda p, b, *_: (0, 0)),
            pl.BlockSpec((1, two), lambda p, b, *_: (0, p)),
            pl.BlockSpec((2, tap_rows, PAD_DIM), lambda p, b, *_: (p, 0, 0)),
            pl.BlockSpec((1, 4, PAD_DIM), lambda p, b, *_: (p, 0, 0)),
        ],
        scratch_shapes=[
            pltpu.VMEM((HALO + length, two), BF16),
            pltpu.VMEM((TOP + length + HALO, two), BF16),
            pltpu.VMEM((TOP + length + HALO, two), BF16),
            pltpu.VMEM((HALO + length, two), F32),
            pltpu.VMEM((TOP + length + HALO, two), F32),
            pltpu.VMEM((TOP + length + HALO, two), F32),
            pltpu.VMEM((most * EXT, n_taps * WIN), BF16),
            pltpu.VMEM((most * EXT, WIN), BF16),
            pltpu.VMEM((2, WIN, n_taps * WIN), F32),
            pltpu.VMEM((2, most, ROWS, WIN), F32),
            pltpu.VMEM((2, n_taps * WIN, WIN), BF16),
            pltpu.VMEM((pairs, 3, length, two), BF16),
            pltpu.VMEM((length, 1), F32),
        ],
    )
    return pl.pallas_call(
        functools.partial(backward_kernel, n_taps, key_half, most),
        grid_spec=grid_spec,
        out_shape=[
            jax.ShapeDtypeStruct((length, 3 * heads * HEAD_DIM), BF16),
            jax.ShapeDtypeStruct((length // ROWS, ROWS), F32),
            jax.ShapeDtypeStruct((1, heads * PAD_DIM), F32),
            jax.ShapeDtypeStruct((heads, tap_rows, PAD_DIM), F32),
            jax.ShapeDtypeStruct((pairs, 4, PAD_DIM), F32),
        ],
        compiler_params=pltpu.CompilerParams(vmem_limit_bytes=56 << 20),
        cost_estimate=COST,
        name="attend_backward",
    )(counts, mix, proj, proj, proj, start, base, gain, probs, heads_out, grad_grouped)


MESH_ID = pl.DeviceIdType.MESH


def ring_place(member, n):
    z, y = member // 2, member % 2
    return (1 - y) * z + y * (n - 1 - z)


def ring_member(place, n):
    upper = place // (n // 2)
    return (1 - upper) * 2 * place + upper * (2 * (n - 1 - place) + 1)


def ring_peers(n):
    place = ring_place(lax.axis_index("dp"), n)
    ahead = ring_member(lax.rem(place + 1, n), n)
    behind = ring_member(lax.rem(place + n - 1, n), n)
    return place, (ahead, behind)


def ring_scratch(arrays, n):
    return [pltpu.VMEM((2, n - 1) + a.shape[2:], a.dtype) for a in arrays] + [
        pltpu.SemaphoreType.DMA((2, len(arrays), n - 1))
    ] * 4


def ring_split(array, n):
    return array.reshape(n, 2, -1, array.shape[-1])


def make_ring(n, sources, ins, outs, scratch):
    count = len(ins)
    slots = scratch[:count]
    rs_send, rs_recv, ag_send, ag_recv = scratch[count:]
    place, to = ring_peers(n)

    def chunk(way, back):
        return lax.rem(place - back + 2 * n if way == 0 else place + back, n)

    def sum_copy(way, k, s, src):
        return pltpu.make_async_remote_copy(
            src_ref=src,
            dst_ref=slots[k].at[way, s],
            send_sem=rs_send.at[way, k, s],
            recv_sem=rs_recv.at[way, k, s],
            device_id={"dp": to[way]},
            device_id_type=MESH_ID,
        )

    def share_copy(way, k, s, c):
        return pltpu.make_async_remote_copy(
            src_ref=outs[k].at[c, way],
            dst_ref=outs[k].at[c, way],
            send_sem=ag_send.at[way, k, s],
            recv_sem=ag_recv.at[way, k, s],
            device_id={"dp": to[way]},
            device_id_type=MESH_ID,
        )

    def add(way, k, s, c, dst):
        total = slots[k][way, s].astype(F32) + ins[k][c, way].astype(F32)
        dst[...] = total.astype(dst.dtype)

    both = [(k, way) for k in range(count) for way in range(2)]

    def start():
        for k, way in both:
            sum_copy(way, k, 0, sources[k].at[chunk(way, 1), way]).start()

    def tick(now):
        @pl.when(now < n - 2)
        def _():
            for k, way in both:
                sum_copy(way, k, now, slots[k].at[way, now]).wait_recv()
                add(way, k, now, chunk(way, 2 + now), slots[k].at[way, now])
                sum_copy(way, k, now + 1, slots[k].at[way, now]).start()

        @pl.when(now == n - 2)
        def _():
            for k, way in both:
                sum_copy(way, k, n - 2, slots[k].at[way, n - 2]).wait_recv()
                add(way, k, n - 2, place, outs[k].at[place, way])
                share_copy(way, k, 0, place).start()

        @pl.when((now > n - 2) & (now < 2 * n - 3))
        def _():
            step = now - (n - 1)
            for k, way in both:
                share_copy(way, k, step, chunk(way, step + 1)).wait_recv()
                share_copy(way, k, step + 1, chunk(way, step + 1)).start()

        @pl.when(now == 2 * n - 3)
        def _():
            for k, way in both:
                share_copy(way, k, n - 2, chunk(way, n - 1)).wait_recv()

    def drain():
        def one(s, carry):
            for k, way in both:
                sum_copy(way, k, s, slots[k].at[way, s]).wait_send()
                share_copy(way, k, s, place).wait_send()
            return carry

        lax.fori_loop(0, n - 1, one, 0)

    return start, tick, drain


def small_rows(size):
    return -(-size // PAD_DIM)


def pack_small(arrays, rows):
    packed = []
    for a in arrays:
        flat = a.reshape(-1)
        packed.append(jnp.pad(flat, (0, -flat.size % PAD_DIM)).reshape(-1, PAD_DIM))
    packed = jnp.concatenate(packed, axis=0)
    return jnp.pad(packed, ((0, rows - packed.shape[0]), (0, 0)))


def unpack_small(packed, arrays):
    found, at = [], 0
    for a in arrays:
        rows = small_rows(a.size)
        found.append(packed[at : at + rows].reshape(-1)[: a.size].reshape(a.shape))
        at += rows
    return found


CHUNK = 128
GROUP = 256


LIVE = 4


def exchange_scratch(steps, width, ranks, share=True, chunk=CHUNK):
    half = ranks // 2
    live = steps if share else LIVE
    shared = [pltpu.VMEM((steps, ranks, chunk, width), BF16)] if share else []
    return [
        pltpu.VMEM((steps, half, chunk, width), BF16),
        pltpu.VMEM((steps, half, chunk, width), BF16),
        pltpu.VMEM((live, half, chunk, width), F32),
        pltpu.VMEM((steps, chunk, width), BF16),
        pltpu.VMEM((steps, chunk, width), BF16),
        pltpu.SemaphoreType.DMA((5, steps)),
        pltpu.SemaphoreType.DMA((5, steps)),
    ] + shared


def tensor_peers():
    me = lax.axis_index("tensor")
    return me, me + 1 - 2 * lax.rem(me, 2), lax.rem(me + 2, 4)


def meet(signals):
    barrier = pltpu.get_barrier_semaphore()
    for device in signals:
        pl.semaphore_signal(barrier, inc=1, device_id=device, device_id_type=MESH_ID)
    pl.semaphore_wait(barrier, len(signals))


def exchange_copies(scratch):
    out_a, in_a, _, out_b, in_b, send, recv, *full = scratch
    me, near, far = tensor_peers()

    def copy(kind, step, src, dst, peer):
        return pltpu.make_async_remote_copy(
            src_ref=src,
            dst_ref=dst,
            send_sem=send.at[kind, step],
            recv_sem=recv.at[kind, step],
            device_id={"tensor": peer},
            device_id_type=MESH_ID,
        )

    def cores(step):
        return copy(0, step, out_a.at[step], in_a.at[step], near)

    def chips(step):
        return copy(1, step, out_b.at[step], in_b.at[step], far)

    def back_far(step):
        return copy(2, step, full[0].at[step, me], full[0].at[step, me], far)

    def back_near(step):
        return copy(3, step, full[0].at[step, me], full[0].at[step, me], near)

    def pass_near(step):
        return copy(4, step, full[0].at[step, far], full[0].at[step, far], near)

    return cores, chips, back_far, back_near, pass_near


def exchange_stages(scratch, partial, live, chunk):
    out_a, in_a, kept, out_b, in_b = scratch[:5]
    cores, chips = exchange_copies(scratch)[:2]
    many = GROUP // chunk
    me, near, far = tensor_peers()

    def begin(step):
        for n, owner in ((0, near), (1, lax.rem(near + 2, 4))):

            def put(term, n=n):
                term = term.astype(BF16)
                for m in range(many):
                    out_a[step + m, n] = term[m * chunk : (m + 1) * chunk]

            partial(step, owner, put)
        for m in range(many):
            cores(step + m).start()
        for n, owner in ((1, far), (0, me)):

            def put(term, n=n):
                for m in range(many):
                    kept[lax.rem(step + m, live), n] = term[m * chunk : (m + 1) * chunk]

            partial(step, owner, put)

    def over(step):
        cores(step).wait_recv()
        out_b[step] = (kept[lax.rem(step, live), 1] + in_a[step, 1].astype(F32)).astype(BF16)
        chips(step).start()

    def total(step):
        chips(step).wait_recv()
        return kept[lax.rem(step, live), 0] + in_a[step, 0].astype(F32) + in_b[step].astype(F32)

    return begin, over, total


def make_exchange(steps, scratch, partial, local, between, chunk):
    cores, chips = exchange_copies(scratch)[:2]
    begin, over, total = exchange_stages(scratch, partial, LIVE, chunk)
    many = GROUP // chunk

    def tick(now):
        @pl.when((lax.rem(now, many) == 0) & (now < steps))
        def _():
            begin(now)

        between(now)

        @pl.when((now >= 1) & (now < steps + 1))
        def _():
            over(now - 1)

        @pl.when((now >= 2) & (now < steps + 2))
        def _():
            local(now - 2, total(now - 2))

    def drain():
        def one(step, carry):
            cores(step).wait_send()
            chips(step).wait_send()
            return carry

        lax.fori_loop(0, steps, one, 0)

    return tick, steps + 2, drain


def run_exchange(steps, scratch, partial, local, whole, beside=None, ahead=None):
    cores, chips, back_far, back_near, pass_near = exchange_copies(scratch)
    begin, over, total = exchange_stages(scratch, partial, steps, CHUNK)
    full = scratch[7]
    many = GROUP // CHUNK
    me = tensor_peers()[0]

    def send_group(group, carry):
        @pl.when(group < steps // many)
        def _():
            begin(group * many)

        @pl.when(group >= 1)
        def _():
            for m in range(many):
                over((group - 1) * many + m)

        return carry

    lax.fori_loop(0, steps // many + 1, send_group, 0)

    def sum_group(group, carry):
        if beside is not None:
            beside(group)
        for m in range(many):
            step = group * many + m
            full[step, me] = local(step, total(step)).astype(BF16)
            back_far(step).start()
            back_near(step).start()
        return carry

    lax.fori_loop(0, steps // many, sum_group, 0)
    if ahead is not None:
        ahead()

    def share_step(now, carry):
        @pl.when(now < steps)
        def _():
            back_far(now).wait_recv()
            pass_near(now).start()

        @pl.when(now >= 1)
        def _():
            back_near(now - 1).wait_recv()
            pass_near(now - 1).wait_recv()
            whole(now - 1, full)

        return carry

    lax.fori_loop(0, steps + 1, share_step, 0)

    def drain(step, carry):
        for copy in (cores, chips, back_far, back_near, pass_near):
            copy(step).wait_send()
        return carry

    lax.fori_loop(0, steps, drain, 0)


def run_ticks(count, *ticks):
    def one(now, carry):
        for tick in ticks:
            tick(now)
        return carry

    lax.fori_loop(0, count, one, 0)


def group_rows(step, chunk=CHUNK):
    return pl.ds(pl.multiple_of(step * chunk, chunk), GROUP)


def owner_cols(owner, width):
    return pl.ds(pl.multiple_of(owner * width, PAD_DIM), width)


def step_rows(step, chunk=CHUNK):
    return pl.ds(pl.multiple_of(step * chunk, chunk), chunk)


def first_entry_kernel(
    tokens_ref, w_ref, gains_ref, proj_ref, normed_ref, factor_ref, gains_all_ref, full, gains_in,
    send, recv, gains_send, gains_recv,
):
    rows, width = tokens_ref.shape
    ranks = normed_ref.shape[1] // width
    heads = width // HEAD_DIM
    steps, many = rows // CHUNK, GROUP // CHUNK
    me, near, far = tensor_peers()
    across = lax.rem(near + 2, 4)
    meet([{"tensor": near}, {"tensor": far}, {"tensor": across}])

    def copy(kind, step, src, dst, peer):
        return pltpu.make_async_remote_copy(
            src_ref=src,
            dst_ref=dst,
            send_sem=send.at[kind, step],
            recv_sem=recv.at[kind, step],
            device_id={"tensor": peer},
            device_id_type=MESH_ID,
        )

    def to_far(step):
        return copy(0, step, tokens_ref.at[step_rows(step)], full.at[step, me], far)

    def to_near(step):
        return copy(1, step, tokens_ref.at[step_rows(step)], full.at[step, me], near)

    def pass_near(step):
        return copy(2, step, full.at[step, far], full.at[step, far], near)

    def gains_copy(kind, peer, sender):
        return pltpu.make_async_remote_copy(
            src_ref=gains_ref,
            dst_ref=gains_in.at[sender],
            send_sem=gains_send.at[kind],
            recv_sem=gains_recv.at[sender],
            device_id={"tensor": peer},
            device_id_type=MESH_ID,
        )

    peers = (near, far, across)
    for kind, peer in enumerate(peers):
        gains_copy(kind, peer, me).start()

    def send_all(step, carry):
        to_far(step).start()
        to_near(step).start()
        full[step, me] = tokens_ref[step_rows(step), :]
        return carry

    lax.fori_loop(0, steps, send_all, 0)
    gains_in[me] = gains_ref[...]
    for kind, peer in enumerate(peers):
        gains_copy(kind, peer, peer).wait()
    for n in range(ranks):
        gains_all_ref[:, n * width : (n + 1) * width] = gains_in[n]

    def tick(now):
        @pl.when(now < steps)
        def _():
            to_far(now).wait_recv()
            pass_near(now).start()

        @pl.when(now >= 1)
        def _():
            to_near(now - 1).wait_recv()
            pass_near(now - 1).wait_recv()

        @pl.when((now >= many) & (lax.rem(now, many) == 0))
        def _():
            first = now - many
            at = group_rows(first)
            blocks = [
                jnp.concatenate([full[first + m, n] for m in range(many)], axis=0).astype(F32)
                for n in range(ranks)
            ]
            squares = sum(jnp.sum(block * block, axis=-1, keepdims=True) for block in blocks)
            factor = lax.rsqrt(squares * (1.0 / (ranks * width)) + EPS)
            factor_ref[at, :] = factor
            for n, block in enumerate(blocks):
                cols = slice(n * width, (n + 1) * width)
                normed_ref[at, cols] = (block * factor * gains_all_ref[0:1, cols]).astype(BF16)
            for c in range(3):
                out = dot_nn(normed_ref[at, :], w_ref[c])
                empty = jnp.zeros((GROUP, PAD_DIM - HEAD_DIM), F32)
                for h in range(heads):
                    head = jnp.concatenate([out[:, h * HEAD_DIM : (h + 1) * HEAD_DIM], empty], axis=1)
                    lane = (c * heads + h) * PAD_DIM
                    proj_ref[at, lane : lane + PAD_DIM] = head.astype(BF16)

    run_ticks(steps + 1, tick)

    def drain(step, carry):
        to_far(step).wait_send()
        to_near(step).wait_send()
        pass_near(step).wait_send()
        return carry

    lax.fori_loop(0, steps, drain, 0)


def first_entry(tokens, w_qkv, gains):
    rows, width = tokens.shape
    full_width = w_qkv.shape[1]
    ranks = full_width // width
    steps = rows // CHUNK
    vmem = pl.BlockSpec(memory_space=pltpu.VMEM)
    return pl.pallas_call(
        first_entry_kernel,
        out_shape=[
            jax.ShapeDtypeStruct((rows, 3 * width // HEAD_DIM * PAD_DIM), BF16),
            jax.ShapeDtypeStruct((rows, full_width), BF16),
            jax.ShapeDtypeStruct((rows, 1), F32),
            jax.ShapeDtypeStruct((8, full_width), F32),
        ],
        in_specs=[vmem] * 3,
        out_specs=[vmem] * 4,
        scratch_shapes=[
            pltpu.VMEM((steps, ranks, CHUNK, width), BF16),
            pltpu.VMEM((ranks, 8, width), F32),
            pltpu.SemaphoreType.DMA((3, steps)),
            pltpu.SemaphoreType.DMA((3, steps)),
            pltpu.SemaphoreType.DMA((3,)),
            pltpu.SemaphoreType.DMA((ranks,)),
        ],
        compiler_params=pltpu.CompilerParams(
            collective_id=4, has_side_effects=True, vmem_limit_bytes=40 << 20
        ),
        cost_estimate=COST,
        name="first_entry",
    )(tokens, w_qkv, gains)


def attn_exit_kernel(
    grouped_ref, w_out_ref, tokens_ref, gain_ref, cot_in, w_gate_up_in, w_down_in, hidden_local_ref,
    hidden_out, normed_out, w_ref, act_out, grad_gate_out, grad_up_out, hidden_ref, normed_ref, act_ref,
    grad_gate_ref, grad_up_ref, grad_act, cot_ref, w_gate_up_ref, w_down_ref, load, store, *scratch
):
    loads = [
        pltpu.make_async_copy(src, dst, load.at[n])
        for n, (src, dst) in enumerate(
            ((cot_in, cot_ref), (w_down_in, w_down_ref), (w_gate_up_in, w_gate_up_ref))
        )
    ]
    for one in loads:
        one.start()
    rows, width = tokens_ref.shape
    ranks = hidden_ref.shape[1] // width
    many = GROUP // CHUNK
    for h in range(width // HEAD_DIM):
        lead = h * PAD_DIM
        w_ref[lead : lead + HEAD_DIM, :] = w_out_ref[h * HEAD_DIM : (h + 1) * HEAD_DIM, :]
        w_ref[lead + HEAD_DIM : lead + PAD_DIM, :] = jnp.zeros((PAD_DIM - HEAD_DIM, w_ref.shape[1]), BF16)

    def partial(step, owner, put):
        put(dot_nn(grouped_ref[group_rows(step), :], w_ref[:, owner_cols(owner, width)]))

    def local(step, total):
        hidden = tokens_ref[step_rows(step), :].astype(F32) + total
        hidden_local_ref[step_rows(step), :] = hidden
        return hidden

    def whole(step, full):
        squares = None
        for n in range(ranks):
            block = full[step, n]
            hidden_ref[step_rows(step), n * width : (n + 1) * width] = block
            block = block.astype(F32)
            part = jnp.sum(block * block, axis=-1, keepdims=True)
            squares = part if squares is None else squares + part
        factor = lax.rsqrt(squares * (1.0 / (ranks * width)) + EPS)
        for n in range(ranks):
            cols = slice(n * width, (n + 1) * width)
            unit = full[step, n].astype(F32) * factor
            normed_ref[step_rows(step), cols] = (unit * gain_ref[:, cols]).astype(BF16)

        @pl.when(lax.rem(step, many) == many - 1)
        def _():
            at = group_rows(step - (many - 1))
            gate = dot_nn(normed_ref[at, :], w_gate_up_ref[0])
            up = dot_nn(normed_ref[at, :], w_gate_up_ref[1])
            sigmoid = jax.nn.sigmoid(gate)
            swish = gate * sigmoid
            grad = grad_act[at, :]
            act_ref[at, :] = (swish * up).astype(BF16)
            grad_gate_ref[at, :] = (grad * up * sigmoid * (1.0 + gate * (1.0 - sigmoid))).astype(BF16)
            grad_up_ref[at, :] = (grad * swish).astype(BF16)
            for one in stores(step // many):
                one.start()

    def stores(group):
        at = group_rows(group * many)
        pairs = (
            (hidden_ref, hidden_out),
            (normed_ref, normed_out),
            (act_ref, act_out),
            (grad_gate_ref, grad_gate_out),
            (grad_up_ref, grad_up_out),
        )
        return [
            pltpu.make_async_copy(src.at[at], dst.at[at], store.at[n, group])
            for n, (src, dst) in enumerate(pairs)
        ]

    def beside(group):
        @pl.when(group == 0)
        def _():
            loads[0].wait()
            loads[1].wait()

        at = group_rows(group * many)
        grad_act[at, :] = dot_nt(cot_ref[at, :], w_down_ref[...])

    me, near, far = tensor_peers()
    meet([{"tensor": near}, {"tensor": far}])
    run_exchange(rows // CHUNK, scratch, partial, local, whole, beside, loads[2].wait)

    def stored(group, carry):
        for one in stores(group):
            one.wait()
        return carry

    lax.fori_loop(0, rows // GROUP, stored, 0)


def attn_exit(grouped, w_out, tokens, gain, full_cot, w_gate_up, w_down):
    rows, width = tokens.shape
    full_width = w_out.shape[1]
    units = w_down.shape[0]
    vmem = pl.BlockSpec(memory_space=pltpu.VMEM)
    anywhere = pl.BlockSpec(memory_space=pl.ANY)
    return pl.pallas_call(
        attn_exit_kernel,
        out_shape=[
            jax.ShapeDtypeStruct((rows, width), F32),
            jax.ShapeDtypeStruct((rows, full_width), BF16),
            jax.ShapeDtypeStruct((rows, full_width), BF16),
            jax.ShapeDtypeStruct((grouped.shape[1], full_width), BF16),
        ]
        + [jax.ShapeDtypeStruct((rows, units), BF16)] * 3,
        in_specs=[vmem] * 4 + [anywhere] * 3,
        out_specs=[vmem, anywhere, anywhere, vmem] + [anywhere] * 3,
        scratch_shapes=[pltpu.VMEM((rows, full_width), BF16)] * 2
        + [pltpu.VMEM((rows, units), BF16)] * 3
        + [
            pltpu.VMEM((rows, units), F32),
            pltpu.VMEM(full_cot.shape, BF16),
            pltpu.VMEM(w_gate_up.shape, BF16),
            pltpu.VMEM(w_down.shape, BF16),
            pltpu.SemaphoreType.DMA((3,)),
            pltpu.SemaphoreType.DMA((5, rows // GROUP)),
        ]
        + exchange_scratch(rows // CHUNK, width, full_width // width),
        compiler_params=pltpu.CompilerParams(
            collective_id=1, has_side_effects=True, vmem_limit_bytes=56 << 20
        ),
        cost_estimate=COST,
        name="attn_exit",
    )(grouped, w_out, tokens, gain, full_cot, w_gate_up, w_down)


def mlp_exit_kernel(
    gate_ref, up_ref, w_ref, hidden_in, cot_in, hidden_local_ref, cot_local_ref, gain_ref, gain_local_ref,
    grad_attn_ref, grad_hidden_ref, gain_grad_ref, grad_local, hidden_ref, cot_ref, load, *scratch
):
    loads = [
        pltpu.make_async_copy(hidden_in, hidden_ref, load.at[0]),
        pltpu.make_async_copy(cot_in, cot_ref, load.at[1]),
    ]
    for one in loads:
        one.start()
    rows, width = cot_local_ref.shape
    full_width = hidden_ref.shape[1]
    ranks = full_width // width
    gain_grad_ref[...] = jnp.zeros_like(gain_grad_ref)

    def partial(step, owner, put):
        cols = owner_cols(owner, width)
        at = group_rows(step)
        put(dot_nt(gate_ref[at, :], w_ref[0, cols, :]) + dot_nt(up_ref[at, :], w_ref[1, cols, :]))

    def local(step, total):
        grad_local[step_rows(step), :] = total
        return total

    def whole(step, full):
        at = step_rows(step)
        squares, inner = None, None
        for n in range(ranks):
            cols = slice(n * width, (n + 1) * width)
            hidden = hidden_ref[at, cols].astype(F32)
            part = jnp.sum(hidden * hidden, axis=-1, keepdims=True)
            squares = part if squares is None else squares + part
            part = jnp.sum(full[step, n].astype(F32) * gain_ref[:, cols] * hidden, axis=-1, keepdims=True)
            inner = part if inner is None else inner + part
        factor = lax.rsqrt(squares * (1.0 / full_width) + EPS)
        inner = inner * factor * (1.0 / full_width)
        for n in range(ranks):
            cols = slice(n * width, (n + 1) * width)
            unit = hidden_ref[at, cols].astype(F32) * factor
            grad = full[step, n].astype(F32) * gain_ref[:, cols] - unit * inner
            grad_attn_ref[at, cols] = (cot_ref[at, cols].astype(F32) + factor * grad).astype(BF16)
        total = grad_local[at, :]
        unit = hidden_local_ref[at, :] * factor
        gain_grad_ref[...] += jnp.sum(total * unit, axis=0, keepdims=True)
        grad_hidden_ref[at, :] = cot_local_ref[at, :].astype(F32) + factor * (
            total * gain_local_ref[...] - unit * inner
        )

    me, near, far = tensor_peers()
    meet([{"tensor": near}, {"tensor": far}])

    def ahead():
        for one in loads:
            one.wait()

    run_exchange(rows // CHUNK, scratch, partial, local, whole, ahead=ahead)


def mlp_exit(grad_gate, grad_up, w_gate_up, hidden, full_cot, hidden_local, cotangent, gain, gain_local):
    rows, width = hidden_local.shape
    full_width = hidden.shape[1]
    vmem = pl.BlockSpec(memory_space=pltpu.VMEM)
    return pl.pallas_call(
        mlp_exit_kernel,
        out_shape=[
            jax.ShapeDtypeStruct((rows, full_width), BF16),
            jax.ShapeDtypeStruct((rows, width), F32),
            jax.ShapeDtypeStruct((1, width), F32),
        ],
        in_specs=[vmem] * 3 + [pl.BlockSpec(memory_space=pl.ANY)] * 2 + [vmem] * 4,
        out_specs=[vmem] * 3,
        scratch_shapes=[
            pltpu.VMEM((rows, width), F32),
            pltpu.VMEM(hidden.shape, BF16),
            pltpu.VMEM(full_cot.shape, BF16),
            pltpu.SemaphoreType.DMA((2,)),
        ]
        + exchange_scratch(rows // CHUNK, width, full_width // width),
        compiler_params=pltpu.CompilerParams(
            collective_id=2, has_side_effects=True, vmem_limit_bytes=56 << 20
        ),
        cost_estimate=COST,
        name="mlp_exit",
    )(grad_gate, grad_up, w_gate_up, hidden, full_cot, hidden_local, cotangent, gain, gain_local)


def last_exit_kernel(
    n_ring, count, factor_ref, inner_ref, gain_ref, small_ref, *refs,
):
    given, sources, refs = refs[:7], refs[7 : 7 + count], refs[7 + count :]
    tokens_grad_ref, out_ref, small_sum_ref = refs[:3]
    outs, refs = refs[3 : 3 + count], refs[3 + count :]
    here_too, ins, load, refs = refs[:7], refs[7 : 7 + count], refs[7 + count], refs[8 + count :]
    grad_ref, w_ref, tokens_ref, grad_hidden_ref, act_ref, w_down_ref, hidden_ref = here_too
    loads = [
        pltpu.make_async_copy(src, dst, load.at[n])
        for n, (src, dst) in enumerate(zip((*sources, *given), (*ins, *here_too)))
    ]
    for one in loads:
        one.start()
    gain_grad, mine, all_small, small_send, small_recv = refs[:5]
    inner_in, inner_sum, inner_col, inner_send, inner_recv = refs[5:10]
    ring_refs, scratch = refs[10 : 14 + count], refs[14 + count :]
    rows, width = tokens_ref.shape
    full_width = w_ref.shape[1]
    half = rows // GROUP
    me, near, far = tensor_peers()
    here = lax.axis_index("dp")
    gain_grad[...] = jnp.zeros_like(gain_grad)

    def partial(step, owner, put):
        cols = owner_cols(owner, width)

        @pl.when(step < half)
        def _():
            total = None
            for c in range(3):
                term = dot_nt(grad_ref[group_rows(step, GROUP), c * width : (c + 1) * width], w_ref[c, cols, :])
                total = term if total is None else total + term
            put(total)

        @pl.when(step >= half)
        def _():
            put(dot_nn(act_ref[group_rows(step - half, GROUP), :], w_down_ref[:, cols]))

    def between(now):
        def copy(n, src, peer):
            return pltpu.make_async_remote_copy(
                src_ref=src,
                dst_ref=inner_in.at[n],
                send_sem=inner_send.at[n],
                recv_sem=inner_recv.at[n],
                device_id={"tensor": peer},
                device_id_type=MESH_ID,
            )

        @pl.when(now == 0)
        def _():
            copy(0, inner_ref, near).start()

        @pl.when(now == 1)
        def _():
            copy(0, inner_ref, near).wait()
            inner_sum[...] = inner_ref[...] + inner_in[0]
            copy(1, inner_sum, far).start()

        @pl.when(now == 2)
        def _():
            copy(1, inner_sum, far).wait()
            total = (inner_sum[...] + inner_in[1]) * (1.0 / full_width)
            for n in range(rows // ROWS):
                line = jnp.broadcast_to(total[n : n + 1, :], (ROWS, ROWS))
                inner_col[n * ROWS : (n + 1) * ROWS, :] = line.T[:, 0:1]

    def local(step, total):
        @pl.when(step < half)
        def _():
            at = step_rows(step, GROUP)
            factor = factor_ref[at, :]
            unit = tokens_ref[at, :].astype(F32) * factor
            gain_grad[...] += jnp.sum(total * unit, axis=0, keepdims=True)
            tokens_grad_ref[at, :] = grad_hidden_ref[at, :] + factor * (
                total * gain_ref[...] - unit * inner_col[at, :]
            )

        @pl.when(step >= half)
        def _():
            at = step_rows(step - half, GROUP)
            out_ref[at, :] = (hidden_ref[at, :] + total).astype(BF16)

    def small_copy(peer, sender):
        return pltpu.make_async_remote_copy(
            src_ref=mine,
            dst_ref=all_small.at[sender],
            send_sem=small_send.at[peer],
            recv_sem=small_recv.at[sender],
            device_id={"dp": peer},
            device_id_type=MESH_ID,
        )

    def small_start(now):
        @pl.when(now == half + 2)
        def _():
            mine[...] = small_ref[...]
            for n in range(width // PAD_DIM):
                mine[n : n + 1, :] = gain_grad[:, n * PAD_DIM : (n + 1) * PAD_DIM]
            all_small[here] = mine[...]

            def one(away, carry):
                small_copy(lax.rem(here + away, n_ring), here).start()
                return carry

            lax.fori_loop(1, n_ring, one, 0)

    barrier = pltpu.get_barrier_semaphore()
    for peer in (near, far):
        pl.semaphore_signal(barrier, inc=1, device_id={"tensor": peer}, device_id_type=MESH_ID)

    def greet(away, carry):
        peer = lax.rem(here + away, n_ring)
        pl.semaphore_signal(barrier, inc=1, device_id={"dp": peer}, device_id_type=MESH_ID)
        return carry

    lax.fori_loop(1, n_ring, greet, 0)
    pl.semaphore_wait(barrier, 2 + n_ring - 1)

    ring_start, ring_tick, ring_drain = make_ring(n_ring, sources, ins, outs, ring_refs)
    tick, ticks, drain = make_exchange(2 * half, scratch, partial, local, between, GROUP)
    ring_start()
    for one in loads:
        one.wait()
    run_ticks(max(ticks, 2 * (n_ring - 1)), ring_tick, tick, small_start)

    def one(away, carry):
        peer = lax.rem(here + away, n_ring)
        small_copy(peer, peer).wait()
        return carry

    lax.fori_loop(1, n_ring, one, 0)

    def add(n, total):
        return total + all_small[n]

    small_sum_ref[...] = lax.fori_loop(1, n_ring, add, all_small[0])
    drain()
    ring_drain()


def last_exit(
    grad_proj, w_qkv, tokens, grad_hidden, factor, inner, gain, act, w_down, hidden_local, small, sums
):
    rows, width = tokens.shape
    n_ring = lax.axis_size("dp")
    count = len(sums)
    split = [ring_split(a, n_ring) for a in sums]
    gain_rows = width // PAD_DIM
    need = gain_rows + sum(small_rows(a.size) for a in small)
    packed = jnp.pad(pack_small(small, need - gain_rows), ((gain_rows, -need % 8), (0, 0)))
    vmem = pl.BlockSpec(memory_space=pltpu.VMEM)
    steps = 2 * rows // GROUP
    given = (grad_proj, w_qkv, tokens, grad_hidden, act, w_down, hidden_local)
    tokens_grad, out, packed, *totals = pl.pallas_call(
        functools.partial(last_exit_kernel, n_ring, count),
        out_shape=[
            jax.ShapeDtypeStruct((rows, width), F32),
            jax.ShapeDtypeStruct((rows, width), BF16),
            jax.ShapeDtypeStruct(packed.shape, F32),
        ]
        + [jax.ShapeDtypeStruct(a.shape, a.dtype) for a in split],
        in_specs=[vmem] * 4 + [pl.BlockSpec(memory_space=pl.ANY)] * (7 + count),
        out_specs=[vmem] * (3 + count),
        scratch_shapes=[pltpu.VMEM(a.shape, a.dtype) for a in (*given, *split)]
        + [
            pltpu.SemaphoreType.DMA((7 + count,)),
            pltpu.VMEM((1, width), F32),
            pltpu.VMEM(packed.shape, F32),
            pltpu.VMEM((n_ring,) + packed.shape, F32),
            pltpu.SemaphoreType.DMA((n_ring,)),
            pltpu.SemaphoreType.DMA((n_ring,)),
            pltpu.VMEM((2,) + inner.shape, F32),
            pltpu.VMEM(inner.shape, F32),
            pltpu.VMEM((rows, 1), F32),
            pltpu.SemaphoreType.DMA((2,)),
            pltpu.SemaphoreType.DMA((2,)),
        ]
        + ring_scratch(split, n_ring)
        + exchange_scratch(steps, width, w_qkv.shape[1] // width, False, GROUP),
        compiler_params=pltpu.CompilerParams(
            collective_id=3, has_side_effects=True, vmem_limit_bytes=62 << 20
        ),
        cost_estimate=COST,
        name="last_exit",
    )(factor, inner, gain, packed, *given, *split)
    gain_grad = packed[:gain_rows].reshape(width)
    totals = [t.reshape(a.shape) for t, a in zip(totals, sums)]
    return tokens_grad, gain_grad, out, unpack_small(packed[gain_rows:], small), totals


def banded(line):
    return pltpu.roll(jnp.broadcast_to(line, (WIN, WIN)), 0, 1, stride=1, stride_axis=0)


def band_lines(kernel):
    taps = kernel.shape[2]
    wide = jnp.pad(kernel, ((0, 0), (0, 0), (0, WIN - taps)))
    back = jnp.pad(kernel[:, :, ::-1], ((0, 0), (0, 0), (0, WIN - taps)))
    return jnp.roll(wide, -(taps // 2), axis=2), jnp.roll(back, -(taps // 2), axis=2)


def pad_heads(array, axis):
    shape = array.shape
    heads = shape[axis] // HEAD_DIM
    split = array.reshape(shape[:axis] + (heads, HEAD_DIM) + shape[axis + 1 :])
    widths = [(0, 0)] * split.ndim
    widths[axis + 1] = (0, PAD_DIM - HEAD_DIM)
    return jnp.pad(split, widths).reshape(shape[:axis] + (heads * PAD_DIM,) + shape[axis + 1 :])


def cut_heads(array, axis):
    shape = array.shape
    heads = shape[axis] // PAD_DIM
    split = array.reshape(shape[:axis] + (heads, PAD_DIM) + shape[axis + 1 :])
    cut = lax.slice_in_dim(split, 0, HEAD_DIM, axis=axis + 1)
    return cut.reshape(shape[:axis] + (heads * HEAD_DIM,) + shape[axis + 1 :])


def windows_needed(start, key_half):
    length = start.shape[0]
    first = start[::ROWS]
    row0 = jnp.arange(0, length, ROWS, dtype=jnp.int32)
    count = jnp.ones_like(first)
    for k in range(1, windows_most(key_half)):
        count = count + (first - key_half < row0 + ROWS - STEP * k).astype(jnp.int32)
    return count


def on_device(
    tokens, segments, attn_gain, w_qkv, kq_kernel, head_mix, group_gain, w_out, mlp_gain, w_gate_up,
    w_down, cotangent,
):
    rows_here, local_width = tokens.shape
    seq_count, length = segments.shape
    heads_here = local_width // HEAD_DIM
    n_taps, key_taps = kq_kernel.shape[1:]
    key_half = key_taps // 2

    lines, lines_back = band_lines(kq_kernel)
    gain_heads = pad_heads(group_gain.astype(F32), 0)[None]
    starts, counts = [], []
    for n in range(seq_count):
        seg = segments[n]
        start = jnp.sum((seg[None, :] < seg[:, None]).astype(jnp.int32), axis=1)
        counts.append(windows_needed(start, key_half))
        starts.append(jnp.pad(start, (HALO, 0), constant_values=1 << 20)[:, None])

    full_width = w_qkv.shape[1]
    own_gains = jnp.pad(jnp.stack([attn_gain, mlp_gain]).astype(F32), ((0, 6), (0, 0)))
    proj, normed_one, scale_one, gains = first_entry(tokens, w_qkv, own_gains)
    gain_two = gains[1:2]
    cot_here, proj = lax.optimization_barrier((cotangent, proj))
    full_cot = lax.all_gather(cot_here, "tensor", axis=1, tiled=True)

    kept = []
    for n in range(seq_count):
        rows = slice(n * length, (n + 1) * length)
        kept.append(
            attend_forward(proj[rows], starts[n], counts[n], lines, head_mix, gain_heads)
        )
    grouped = jnp.concatenate([one[2] for one in kept], axis=0)
    grouped, full_cot = lax.optimization_barrier((grouped, full_cot))
    hidden_local, hidden, normed_two, w_out_pad, act, grad_gate, grad_up = attn_exit(
        grouped, w_out, tokens, gain_two, full_cot, w_gate_up, w_down
    )

    grad_down = dot_tn(act, full_cot).astype(BF16)
    early_rows = int(full_width * EARLY_SHARE)
    early_up = dot_tn(normed_two[:, :early_rows], grad_up).astype(BF16)
    grad_gate, early_up, grad_down = lax.optimization_barrier((grad_gate, early_up, grad_down))
    early_up, grad_down = lax.psum((early_up, grad_down), "dp")
    grad_attn, grad_hidden_local, grad_gain_two = mlp_exit(
        grad_gate, grad_up, w_gate_up, hidden, full_cot, hidden_local, cotangent, gain_two,
        mlp_gain.astype(F32)[None],
    )
    grad_gate_w = dot_tn(normed_two, grad_gate).astype(BF16)
    late_up = dot_tn(normed_two[:, early_rows:], grad_up).astype(BF16)
    grad_w_out = cut_heads(dot_tn(grouped, grad_attn).astype(BF16), 0)

    grad_grouped = dot_nt(grad_attn, w_out_pad)
    parts = []
    for n in range(seq_count):
        rows = slice(n * length, (n + 1) * length)
        parts.append(
            attend_backward(
                proj[rows], starts[n], counts[n], lines_back, head_mix, gain_heads, kept[n][0], kept[n][1],
                grad_grouped[rows],
            )
        )
    grad_proj = jnp.concatenate([one[0] for one in parts], axis=0)
    inner_part = jnp.concatenate([one[1] for one in parts], axis=0)
    grad_group_gain = sum(cut_heads(one[2][0], 0) for one in parts)
    grad_kernel = sum(one[3][:, :, 0] for one in parts).reshape(heads_here, n_taps, key_taps)
    grad_mix = sum(one[4][:, :, 0] for one in parts).reshape(heads_here, 2)

    grad_qkv = [
        dot_tn(normed_one, grad_proj[:, c * local_width : (c + 1) * local_width]).astype(BF16)
        for c in range(3)
    ]
    tokens_grad, grad_gain_one, layer_out, small, sums = last_exit(
        grad_proj, w_qkv, tokens, grad_hidden_local, scale_one, inner_part, attn_gain.astype(F32)[None],
        act, w_down, hidden_local, (grad_kernel, grad_mix, grad_group_gain, grad_gain_two[0]),
        (grad_gate_w, late_up, grad_w_out, *grad_qkv),
    )
    grad_kernel, grad_mix, grad_group_gain, grad_gain_two = small
    grad_gate_w, late_up, grad_w_out, *grad_qkv = sums
    grad_gate_up = jnp.stack([grad_gate_w, jnp.concatenate([early_up, late_up], axis=0)])
    grad_qkv = jnp.stack(grad_qkv)
    return (
        layer_out,
        tokens_grad,
        grad_gain_one,
        grad_qkv.astype(F32),
        grad_kernel,
        grad_mix,
        grad_group_gain,
        grad_w_out.astype(F32),
        grad_gain_two,
        grad_gate_up.astype(F32),
        grad_down.astype(F32),
    )


def solution(mesh):
    in_specs = (
        P("dp", "tensor"),
        P("dp", None),
        P("tensor"),
        P(None, None, "tensor"),
        P("tensor", None, None),
        P("tensor", None),
        P("tensor"),
        P("tensor", None),
        P("tensor"),
        P(None, None, "tensor"),
        P("tensor", None),
        P("dp", "tensor"),
    )
    out_specs = (
        P("dp", "tensor"),
        P("dp", "tensor"),
        P("tensor"),
        P(None, None, "tensor"),
        P("tensor", None, None),
        P("tensor", None),
        P("tensor"),
        P("tensor", None),
        P("tensor"),
        P(None, None, "tensor"),
        P("tensor", None),
    )
    return jax.shard_map(
        on_device, mesh=mesh, in_specs=in_specs, out_specs=out_specs, check_vma=False
    )
```

profile of v0, /device:TPU:0, one launch (start us, length us, event | category | flops | bytes accessed | tf_op | source)
XLA Modules:
  0.0 539.0 jit_solution(13074079114643911543)
XLA Ops:
  7.3 0.7 stack.19
  7.9 0.7 stack.18
  8.7 2.0 copy-done.1
  10.6 1.1 copy-done.2
  11.8 24.6 %first_entry.1 = (bf16[1024,1536]{1,0:T(8,128)(2,1)S(1)}, bf16[1024,1536]{1,0:T(8,128)(2,1)S(1)}, f32[1024,1]{1,0:T(8,128)S(1)}, f32[8,1536]{1,0:T(8,128)S(1)}) custom-call(bf16[1024,384]{1,0:T(8,128)(2,1)S(1)} %copy-done.2, bf16[3,1536,384]{2,1,0:T(8,128)(2,1)S(1)} %copy-done.1, f32[8,384]{1,0:T(8,128)S(1)} %fusion.9.gains_ref), custom_call_target="tpu_custom_call" | custom-call | flops 1048576 | bytes 1024 | tf_op jit(solution)/shard_map/first_entry/pallas_call | solution.py:868
  36.4 1.7 copy-done
  38.1 0.8 copy-done.3
  38.9 0.6 convert_reduce_fusion
  39.6 0.7 copy.46.mix_ref
  40.3 1.0 broadcast_in_dim.12.start_ref
  41.7 0.6 slice.84.gain_ref
  42.3 0.6 pad_convert_fusion
  42.9 0.7 pad_maximum_fusion.1.base_ref
  43.6 0.5 fusion.11.count_ref
  44.1 39.7 %attend_forward.1 = (f32[4,8,3,128,256]{4,3,2,1,0:T(8,128)}, f32[1024,512]{1,0:T(8,128)}, bf16[1024,512]{1,0:T(8,128)(2,1)}) custom-call(s32[8]{0:T(128)} %fusion.11.count_ref, f32[4,2]{1,0:T(4,128)} %copy.46.mix_ref, bf16[1024,1536]{1,0:T(8,128)(2,1)} %copy-done, bf16[1024,1536]{1,0:T(8,128)(2,1)} %copy-done, bf16[1024,1536]{1,0:T(8,128)(2,1)} %copy-done, ...), custom_call_target="tpu_custom_call" | custom-call | flops 1048576 | bytes 1024 | tf_op jit(solution)/shard_map/attend_forward/pallas_call | solution.py:191
  83.9 0.6 reshape_convert_fusion.gain_local_ref
  84.5 47.7 %attn_exit.1 = (f32[1024,384]{1,0:T(8,128)}, bf16[1024,1536]{1,0:T(8,128)(2,1)}, bf16[1024,1536]{1,0:T(8,128)(2,1)}, bf16[512,1536]{1,0:T(8,128)(2,1)}, bf16[102...) custom-call(bf16[1024,512]{1,0:T(8,128)(2,1)} %get-tuple-element.56.grouped_ref, ...), custom_call_target="tpu_custom_call" | custom-call | flops 1048576 | bytes 1024 | tf_op jit(solution)/shard_map/attn_exit/pallas_call | solution.py:992
  132.3 6.7 %convolution_convert_fusion.2 = bf16[1024,1536]{1,0:T(8,128)(2,1)} fusion(bf16[1024,1024]{1,0:T(8,128)(2,1)} %get-tuple-element.62.refs_4_, bf16[1024,1536]{1,0:T(8,128)(2,1)S(1)} %copy-done.4), kind=kOutput, calls=%fused_computation.4 | convolution fusion | flops 3222798336 | bytes 8388608 | tf_op jit(solution)/shard_map/dot_general | solution.py:39
  139.0 4.4 convolution_convert_fusion
  143.5 0.7 copy-done.19
  144.1 0.6 reshape_convert_fusion.1.gain_ref
  144.7 0.7 pad_maximum_fusion.base_ref
  145.4 52.1 %mlp_exit.1 = (bf16[1024,1536]{1,0:T(8,128)(2,1)}, f32[1024,384]{1,0:T(8,128)}, f32[1,384]{1,0:T(1,128)}) custom-call(bf16[1024,1024]{1,0:T(8,128)(2,1)} %get-tuple-element.63.gate_ref, bf16[1024,1024]{1,0:T(8,128)(2,1)} %get-tuple-element.61.up_ref, bf16[2,1536,1024]{2,1,0:T(8,128)(2,1)} %w_ref.3, bf16[1024,1536]{1,0:T(8,128)(2,1)} %get-tuple-element.64.hidden_in, ...), custom_call_target="tpu_custom_call" | custom-call | flops 1048576 | bytes 1024 | tf_op jit(solution)/shard_map/mlp_exit/pallas_call | solution.py:1084
  197.5 5.0 fusion.13.grad_ref
  202.5 66.4 %attend_backward.1 = (bf16[1024,1152]{1,0:T(8,128)(2,1)}, f32[8,128]{1,0:T(8,128)}, f32[1,512]{1,0:T(1,128)}, f32[4,66,128]{2,1,0:T(8,128)}, f32[2,4,128]{2,1,0:T(4,128)}) custom-call(s32[8]{0:T(128)} %fusion.11.count_ref, f32[4,2]{1,0:T(4,128)} %copy.46.mix_ref, bf16[1024,1536]{1,0:T(8,128)(2,1)} %copy-done, bf16[1024,1536]{1,0:T(8,128)(2,1)} %copy-done, ...), custom_call_target="tpu_custom_call" | custom-call | flops 1048576 | bytes 1024 | tf_op jit(solution)/shard_map/attend_backward/pallas_call | solution.py:400
  268.9 0.8 reshape.90
  269.7 0.8 slice_reduce_fusion.1
  270.6 1.1 slice_reduce_fusion
  271.7 4.9 convolution_convert_fusion.3
  276.6 1.1 slice.102
  277.7 0.6 select_maximum_fusion.small_ref
  278.3 3.8 convolution_convert_fusion.7
  282.1 2.9 convolution_convert_fusion.6
  285.0 2.9 convolution_convert_fusion.5
  287.9 2.9 convolution_convert_fusion.4
  290.7 4.8 convolution_convert_fusion.1
  295.6 210.4 %last_exit.1 = (f32[1024,384]{1,0:T(8,128)}, bf16[1024,384]{1,0:T(8,128)(2,1)}, f32[16,128]{1,0:T(8,128)}, bf16[8,2,96,1024]{3,2,1,0:T(8,128)(2,1)}, bf16[8,2,24...) custom-call(f32[1024,1]{1,0:T(8,128)} %copy-done.3, ...), custom_call_target="tpu_custom_call" | custom-call | flops 1048576 | bytes 1024 | tf_op jit(solution)/shard_map/last_exit/pallas_call | solution.py:1263
  505.9 1.4 slice_bitcast_fusion
  507.4 0.6 copy.48
  508.0 0.7 slice_reduce_fusion.2
  508.8 0.7 copy.49
  509.5 5.6 %maximum_convert_fusion.1 = f32[3,1536,384]{2,1,0:T(8,128)} fusion(bf16[1,1536,384]{2,1,0:T(8,128)(2,1)} %bitcast.57, bf16[1,1536,384]{2,1,0:T(8,128)(2,1)} %bitcast.56, bf16[1,1536,384]{2,1,0:T(8,128)(2,1)} %bitcast.55), kind=kLoop, calls=%fused_computation.5 | loop fusion | flops 5308416 | bytes 10616832 | tf_op jit(solution)/shard_map/convert_element_type | solution.py:1422
  515.0 1.8 bitcast_convert_fusion
  516.8 5.6 %convert_element_type.80 = f32[1024,1536]{1,0:T(8,128)} convert(bf16[1024,1536]{1,0:T(8,128)(2,1)} %get-tuple-element.121) | non-fusion elementwise | flops 1572864 | bytes 9437184 | tf_op jit(solution)/shard_map/convert_element_type | solution.py:1429
  522.8 1.6 copy-done.6
  524.3 5.6 %maximum_convert_fusion = f32[2,1536,1024]{2,1,0:T(8,128)} fusion(bf16[1,1536,1024]{2,1,0:T(8,128)(2,1)S(1)} %maximum_bitcast_fusion, bf16[1,1536,1024]{2,1,0:T(8,128)(2,1)S(1)} %bitcast.50), kind=kLoop, calls=%fused_computation | loop fusion | flops 6291456 | bytes 18874368 | tf_op jit(solution)/shard_map/convert_element_type | solution.py:1428
  529.9 0.9 copy.54
  530.8 1.1 copy.55
  (66 shorter events, 1.5 us)
Async XLA Ops:
  7.2 31.8 %copy-start.16 = (s32[1,1024]{1,0:T(1,128)S(1)}, s32[1,1024]{1,0:T(1,128)}, u32[]{:S(2)}) copy-start(s32[1,1024]{1,0:T(1,128)} %param.13) | copy-start | bytes 12292
  7.2 32.4 %copy-start.21 = (f32[4,2]{0,1:T(2,128)S(1)}, f32[4,2]{0,1:T(2,128)}, u32[]{:S(2)}) copy-start(f32[4,2]{0,1:T(2,128)} %param.17) | copy-start | bytes 100
  7.2 34.2 %copy-start.17 = (f32[4,6,11]{2,0,1:T(4,128)S(1)}, f32[4,6,11]{2,0,1:T(4,128)}, u32[]{:S(2)}) copy-start(f32[4,6,11]{2,0,1:T(4,128)} %param.16) | copy-start | bytes 3172
  7.2 34.4 %copy-start.22 = (bf16[384]{0:T(512)(128)(2,1)S(1)}, bf16[384]{0:T(512)(128)(2,1)}, u32[]{:S(2)}) copy-start(bf16[384]{0:T(512)(128)(2,1)} %param.18) | copy-start | bytes 2308
  7.2 77.3 %all-gather.2.cloned.1.call-start = ((), (), s32[]{:S(2)}) async-start(), calls=%async_computation | async-start | bytes 3932160 | tf_op jit(solution)/shard_map/all_gather | solution.py:1362
  8.6 2.0 copy-start.1
  10.6 1.1 copy-start.2
  36.4 1.7 copy-start
  38.1 0.8 copy-start.3
  38.9 477.9 %all-reduce.11.cloned.1.call-start = ((), (), s32[]{:S(2)}) async-start(), calls=%async_computation.1 | async-start | bytes 11010048 | tf_op jit(solution)/shard_map/psum | solution.py:1380
  44.1 39.8 %copy-start.18 = (bf16[384]{0:T(512)(128)(2,1)S(1)}, bf16[384]{0:T(512)(128)(2,1)}, u32[]{:S(2)}) copy-start(bf16[384]{0:T(512)(128)(2,1)} %param.20) | copy-start | bytes 2308
  84.5 47.7 %copy-start.4 = (bf16[1024,1536]{1,0:T(8,128)(2,1)S(1)}, bf16[1024,1536]{1,0:T(8,128)(2,1)}, u32[]{:S(2)}) copy-start(bf16[1024,1536]{1,0:T(8,128)(2,1)} %all-gather.2.cloned.1.call-done.cot_in) | copy-start | bytes 9437188
  132.2 6.8 %copy-start.5 = (bf16[1024,1024]{1,0:T(8,128)(2,1)S(1)}, bf16[1024,1024]{1,0:T(8,128)(2,1)}, u32[]{:S(2)}) copy-start(bf16[1024,1024]{1,0:T(8,128)(2,1)} %get-tuple-element.61.up_ref) | copy-start | bytes 6291460
  132.3 6.8 %copy-start.14 = (bf16[1024,1536]{1,0:T(8,128)(2,1)S(1)}, bf16[1024,1536]{1,0:T(8,128)(2,1)}, u32[]{:S(2)}) copy-start(bf16[1024,1536]{1,0:T(8,128)(2,1)} %get-tuple-element.60) | copy-start | bytes 9437188
  143.4 0.7 copy-start.19
  145.4 52.1 %copy-start.23 = (bf16[512,1536]{1,0:T(8,128)(2,1)S(1)}, bf16[512,1536]{1,0:T(8,128)(2,1)}, u32[]{:S(2)}) copy-start(bf16[512,1536]{1,0:T(8,128)(2,1)} %get-tuple-element.67) | copy-start | bytes 4718596
  271.7 6.0 %copy-start.20 = (f32[1,384]{1,0:T(1,128)S(1)}, f32[1,384]{1,0:T(1,128)}, u32[]{:S(2)}) copy-start(f32[1,384]{1,0:T(1,128)} %get-tuple-element.72) | copy-start | bytes 4612
  277.7 4.4 copy-start.8
  287.8 2.9 copy-start.9
  287.9 2.9 copy-start.15
  509.5 5.6 %copy-start.11 = (bf16[8,2,24,1536]{3,2,1,0:T(8,128)(2,1)S(1)}, bf16[8,2,24,1536]{3,2,1,0:T(8,128)(2,1)}, u32[]{:S(2)}) copy-start(bf16[8,2,24,1536]{3,2,1,0:T(8,128)(2,1)} %get-tuple-element.82) | copy-start | bytes 3538948
  516.8 5.6 %copy-start.7 = (bf16[1152,1024]{1,0:T(8,128)(2,1)S(1)}, bf16[1152,1024]{1,0:T(8,128)(2,1)}, u32[]{:S(2)}) copy-start(bf16[1152,1024]{1,0:T(8,128)(2,1)} %get-tuple-element.120) | copy-start | bytes 7077892
  516.8 5.6 %copy-start.12 = (bf16[8,2,24,1024]{3,2,1,0:T(8,128)(2,1)S(1)}, bf16[8,2,24,1024]{3,2,1,0:T(8,128)(2,1)}, u32[]{:S(2)}) copy-start(bf16[8,2,24,1024]{3,2,1,0:T(8,128)(2,1)} %get-tuple-element.85) | copy-start | bytes 2359300
  522.4 1.9 copy-start.6
  524.3 5.6 %copy-start.13 = (bf16[1024,384]{1,0:T(8,128)(2,1)S(1)}, bf16[1024,384]{1,0:T(8,128)(2,1)}, u32[]{:S(2)}) copy-start(bf16[1024,384]{1,0:T(8,128)(2,1)} %get-tuple-element.139) | copy-start | bytes 2359300
  524.3 6.5 %copy-start.10 = (f32[1024,384]{1,0:T(8,128)S(1)}, f32[1024,384]{1,0:T(8,128)}, u32[]{:S(2)}) copy-start(f32[1024,384]{1,0:T(8,128)} %get-tuple-element.140) | copy-start | bytes 4718596
Sparse Core Ops, SparseCore 0:
  39.0 30.2 all-gather.1
  143.6 217.0 all-reduce.10
where the time goes:
time: 543 us; the launch traced here: 539 us
  Pallas kernels  441 us (81%)
  matrix products  38.2 us (7%)
  other arithmetic  23.7 us (4%)
  local copies, waits for them, and re-layouts  21.6 us (4%)
  between operations  14.5 us (3%)
    pallas_call x1, Pallas kernels, last_exit(): pl.pallas_call(functools.partial(last_exit_kernel, n_ring, count), out_sh...  210 us
    pallas_call x1, Pallas kernels, attend_backward(): pl.pallas_call(functools.partial(backward_kernel, n_taps, key_half, most)...  66.4 us
    pallas_call x1, Pallas kernels, mlp_exit(): pl.pallas_call(mlp_exit_kernel, out_shape=[jax.ShapeDtypeStruct((rows, fu...  52.1 us
    pallas_call x1, Pallas kernels, attn_exit(): pl.pallas_call(attn_exit_kernel, out_shape=[jax.ShapeDtypeStruct((rows, w...  47.7 us
    pallas_call x1, Pallas kernels, attend_forward(): pl.pallas_call(functools.partial(forward_kernel, n_taps, key_half, most),...  39.7 us
    dot_general x8, matrix products, dot_tn(): lax.dot_general(a, b, (((0,), (0,)), ((), ())), preferred_element_type=F32)  33.2 us
    pallas_call x1, Pallas kernels, first_entry(): pl.pallas_call(first_entry_kernel, out_shape=[jax.ShapeDtypeStruct((rows,...  24.6 us
    unnamed x54, local copies, waits for them, and re-layouts  11.9 us
  transfers between devices with their start and end apart: 2, of which 0 were waited for; matrix products, arithmetic and copies ran while one was open for 9% of the time, Pallas kernels for 68%

commit v1 on v0

--- a/solution.py
+++ b/solution.py
@@ -76,7 +76,7 @@
         fill_padded(vs, v_ref, TOP, length)
         for s in range(2):
             for a in range(n_taps):
-                band = banded(base_ref[s, a : a + 1, :])
+                band = banded(band_line(base_ref[s, a : a + 1, :], key_half, 1))
                 high = band.astype(BF16)
                 band_ref[s, a, 0:WIN] = high
                 band_ref[s, a, WIN : 2 * WIN] = high
@@ -152,7 +152,7 @@
             grouped_ref[:, cols] = (out * factor * gain_ref[:, cols]).astype(BF16)
 
     for n in range(1, most + 1):
-        pl.when(count_ref[block] == n)(functools.partial(body, n))
+        pl.when(count_ref[0, block] == n)(functools.partial(body, n))
 
 
 def attend_forward(proj, start, counts, base, mix, gain):
@@ -171,7 +171,7 @@
             pl.BlockSpec((length, two), lambda p, b, *_: (0, pairs + p)),
             pl.BlockSpec((length, two), lambda p, b, *_: (0, 2 * pairs + p)),
             pl.BlockSpec((HALO + length, 1), lambda p, b, *_: (0, 0)),
-            pl.BlockSpec((2, n_taps, WIN), lambda p, b, *_: (p, 0, 0)),
+            pl.BlockSpec((2,) + base.shape[1:], lambda p, b, *_: (p, 0, 0)),
             pl.BlockSpec((1, two), lambda p, b, *_: (0, p)),
         ],
         out_specs=[
@@ -225,7 +225,9 @@
         mix_grad_ref[...] = jnp.zeros_like(mix_grad_ref)
         for s in range(2):
             for a in range(n_taps):
-                t_back_ref[s, a * WIN : (a + 1) * WIN, :] = banded(base_ref[s, a : a + 1, :]).astype(BF16)
+                t_back_ref[s, a * WIN : (a + 1) * WIN, :] = banded(
+                    band_line(base_ref[s, a : a + 1, :], key_half, -1)
+                ).astype(BF16)
 
     row0 = pl.multiple_of(block * ROWS, ROWS)
 
@@ -297,7 +299,7 @@
             tap_sum[s] += dot_tn(inputs[0 : n * EXT, :], taps[0 : n * EXT, :])
 
     for n in range(1, most + 1):
-        pl.when(count_ref[block] == n)(functools.partial(body, n))
+        pl.when(count_ref[0, block] == n)(functools.partial(body, n))
 
     @pl.when(block == pl.num_programs(1) - 1)
     def _():
@@ -368,7 +370,7 @@
             pl.BlockSpec((length, two), lambda p, b, *_: (0, pairs + p)),
             pl.BlockSpec((length, two), lambda p, b, *_: (0, 2 * pairs + p)),
             pl.BlockSpec((HALO + length, 1), lambda p, b, *_: (0, 0)),
-            pl.BlockSpec((2, n_taps, WIN), lambda p, b, *_: (p, 0, 0)),
+            pl.BlockSpec((2,) + base.shape[1:], lambda p, b, *_: (p, 0, 0)),
             pl.BlockSpec((1, two), lambda p, b, *_: (0, p)),
             pl.BlockSpec((2, 1, most, ROWS, WIN), lambda p, b, *_: (p, b, 0, 0, 0)),
             pl.BlockSpec((ROWS, two), lambda p, b, *_: (b, p)),
@@ -758,9 +760,11 @@
 
 
 def first_entry_kernel(
-    tokens_ref, w_ref, gains_ref, proj_ref, normed_ref, factor_ref, gains_all_ref, full, gains_in,
-    send, recv, gains_send, gains_recv,
+    key_half, tokens_ref, w_in, gains_ref, segments_ref, proj_out, normed_out, factor_ref, gains_all_ref, gain_heads_ref,
+    start_ref, count_ref, w_ref, proj_ref, normed_ref, load, store, full, gains_in, send, recv, gains_send, gains_recv,
 ):
+    weights = pltpu.make_async_copy(w_in, w_ref, load.at[0])
+    weights.start()
     rows, width = tokens_ref.shape
     ranks = normed_ref.shape[1] // width
     heads = width // HEAD_DIM
@@ -814,6 +818,36 @@
         gains_copy(kind, peer, peer).wait()
     for n in range(ranks):
         gains_all_ref[:, n * width : (n + 1) * width] = gains_in[n]
+
+    def stores(group):
+        at = group_rows(group * many)
+        return [
+            pltpu.make_async_copy(src.at[at], dst.at[at], store.at[n, group])
+            for n, (src, dst) in enumerate(((proj_ref, proj_out), (normed_ref, normed_out)))
+        ]
+
+    weights.wait()
+    for h in range(heads):
+        own = gains_ref[2:3, h * HEAD_DIM : (h + 1) * HEAD_DIM]
+        gain_heads_ref[:, h * PAD_DIM : (h + 1) * PAD_DIM] = jnp.concatenate(
+            [own, jnp.zeros((1, PAD_DIM - HEAD_DIM), F32)], axis=1
+        )
+    seqs, length = segments_ref.shape
+    for n in range(seqs):
+        lead = n * (HALO + length)
+        start_ref[lead : lead + HALO, :] = jnp.full((HALO, 1), 1 << 20, jnp.int32)
+        line = segments_ref[n : n + 1, :].astype(F32)
+        for b in range(length // ROWS):
+            column = jnp.broadcast_to(line[:, b * ROWS : (b + 1) * ROWS], (ROWS, ROWS)).T[:, 0:1]
+            before = jnp.sum(jnp.where(line < column, 1.0, 0.0), axis=1, keepdims=True)
+            at = lead + HALO + b * ROWS
+            before = before.astype(jnp.int32)
+            start_ref[at : at + ROWS, :] = before
+            count = jnp.ones((1, 1), jnp.int32)
+            for k in range(1, windows_most(key_half)):
+                reach = b * ROWS + ROWS - STEP * k + key_half
+                count = count + jnp.where(before[0:1] < reach, 1, 0)
+            count_ref[n : n + 1, b : b + 1] = count
 
     def tick(now):
         @pl.when(now < steps)
@@ -847,8 +881,17 @@
                     head = jnp.concatenate([out[:, h * HEAD_DIM : (h + 1) * HEAD_DIM], empty], axis=1)
                     lane = (c * heads + h) * PAD_DIM
                     proj_ref[at, lane : lane + PAD_DIM] = head.astype(BF16)
+            for one in stores(first // many):
+                one.start()
 
     run_ticks(steps + 1, tick)
+
+    def stored(group, carry):
+        for one in stores(group):
+            one.wait()
+        return carry
+
+    lax.fori_loop(0, steps // many, stored, 0)
 
     def drain(step, carry):
         to_far(step).wait_send()
@@ -859,23 +902,33 @@
     lax.fori_loop(0, steps, drain, 0)
 
 
-def first_entry(tokens, w_qkv, gains):
+def first_entry(tokens, w_qkv, gains, segments, key_half):
     rows, width = tokens.shape
     full_width = w_qkv.shape[1]
     ranks = full_width // width
     steps = rows // CHUNK
+    padded = 3 * width // HEAD_DIM * PAD_DIM
     vmem = pl.BlockSpec(memory_space=pltpu.VMEM)
+    anywhere = pl.BlockSpec(memory_space=pl.ANY)
     return pl.pallas_call(
-        first_entry_kernel,
+        functools.partial(first_entry_kernel, key_half),
         out_shape=[
-            jax.ShapeDtypeStruct((rows, 3 * width // HEAD_DIM * PAD_DIM), BF16),
+            jax.ShapeDtypeStruct((rows, padded), BF16),
             jax.ShapeDtypeStruct((rows, full_width), BF16),
             jax.ShapeDtypeStruct((rows, 1), F32),
             jax.ShapeDtypeStruct((8, full_width), F32),
+            jax.ShapeDtypeStruct((1, width // HEAD_DIM * PAD_DIM), F32),
+            jax.ShapeDtypeStruct((segments.shape[0] * (HALO + segments.shape[1]), 1), jnp.int32),
+            jax.ShapeDtypeStruct((segments.shape[0], segments.shape[1] // ROWS), jnp.int32),
         ],
-        in_specs=[vmem] * 3,
-        out_specs=[vmem] * 4,
+        in_specs=[vmem, anywhere, vmem, vmem],
+        out_specs=[anywhere, anywhere] + [vmem] * 5,
         scratch_shapes=[
+            pltpu.VMEM(w_qkv.shape, BF16),
+            pltpu.VMEM((rows, padded), BF16),
+            pltpu.VMEM((rows, full_width), BF16),
+            pltpu.SemaphoreType.DMA((1,)),
+            pltpu.SemaphoreType.DMA((2, rows // GROUP)),
             pltpu.VMEM((steps, ranks, CHUNK, width), BF16),
             pltpu.VMEM((ranks, 8, width), F32),
             pltpu.SemaphoreType.DMA((3, steps)),
@@ -884,11 +937,11 @@
             pltpu.SemaphoreType.DMA((ranks,)),
         ],
         compiler_params=pltpu.CompilerParams(
-            collective_id=4, has_side_effects=True, vmem_limit_bytes=40 << 20
+            collective_id=4, has_side_effects=True, vmem_limit_bytes=60 << 20
         ),
         cost_estimate=COST,
         name="first_entry",
-    )(tokens, w_qkv, gains)
+    )(tokens, w_qkv, gains, segments)
 
 
 def attn_exit_kernel(
@@ -932,7 +985,7 @@
         for n in range(ranks):
             cols = slice(n * width, (n + 1) * width)
             unit = full[step, n].astype(F32) * factor
-            normed_ref[step_rows(step), cols] = (unit * gain_ref[:, cols]).astype(BF16)
+            normed_ref[step_rows(step), cols] = (unit * gain_ref[1:2, cols]).astype(BF16)
 
         @pl.when(lax.rem(step, many) == many - 1)
         def _():
@@ -1051,14 +1104,14 @@
             hidden = hidden_ref[at, cols].astype(F32)
             part = jnp.sum(hidden * hidden, axis=-1, keepdims=True)
             squares = part if squares is None else squares + part
-            part = jnp.sum(full[step, n].astype(F32) * gain_ref[:, cols] * hidden, axis=-1, keepdims=True)
+            part = jnp.sum(full[step, n].astype(F32) * gain_ref[1:2, cols] * hidden, axis=-1, keepdims=True)
             inner = part if inner is None else inner + part
         factor = lax.rsqrt(squares * (1.0 / full_width) + EPS)
         inner = inner * factor * (1.0 / full_width)
         for n in range(ranks):
             cols = slice(n * width, (n + 1) * width)
             unit = hidden_ref[at, cols].astype(F32) * factor
-            grad = full[step, n].astype(F32) * gain_ref[:, cols] - unit * inner
+            grad = full[step, n].astype(F32) * gain_ref[1:2, cols] - unit * inner
             grad_attn_ref[at, cols] = (cot_ref[at, cols].astype(F32) + factor * grad).astype(BF16)
         total = grad_local[at, :]
         unit = hidden_local_ref[at, :] * factor
@@ -1297,24 +1350,85 @@
     return tokens_grad, gain_grad, out, unpack_small(packed[gain_rows:], small), totals
 
 
+def widen_kernel(
+    early_steps, gate_ref, early_ref, late_ref, down_ref, out_ref, query_ref, key_ref, value_ref,
+    tokens_ref, layer_ref, gate_up_to, down_to, out_to, qkv_to, tokens_to, layer_to,
+):
+    step = pl.program_id(0)
+    tokens_to[...] = tokens_ref[...]
+    layer_to[...] = layer_ref[...]
+    gate_up_to[0] = gate_ref[...].astype(F32)
+
+    @pl.when(step < early_steps)
+    def _():
+        gate_up_to[1] = early_ref[...].astype(F32)
+
+    @pl.when(step >= early_steps)
+    def _():
+        gate_up_to[1] = late_ref[...].astype(F32)
+
+    down_to[...] = down_ref[...].astype(F32)
+    out_to[...] = out_ref[...].astype(F32)
+    for c, ref in enumerate((query_ref, key_ref, value_ref)):
+        qkv_to[c] = ref[...].astype(F32)
+
+
+def widen(gate, early_up, late_up, down, out, query, key, value, tokens_grad, layer_out):
+    steps = 8
+    full_width, units = gate.shape
+    rows = full_width // steps
+    early_steps = early_up.shape[0] // rows
+    width = query.shape[1]
+
+    def block(array):
+        return pl.BlockSpec((array.shape[0] // steps, array.shape[1]), lambda i: (i, 0))
+
+    return pl.pallas_call(
+        functools.partial(widen_kernel, early_steps),
+        grid=(steps,),
+        out_shape=[
+            jax.ShapeDtypeStruct((2, full_width, units), F32),
+            jax.ShapeDtypeStruct(down.shape, F32),
+            jax.ShapeDtypeStruct(out.shape, F32),
+            jax.ShapeDtypeStruct((3, full_width, width), F32),
+            jax.ShapeDtypeStruct(tokens_grad.shape, tokens_grad.dtype),
+            jax.ShapeDtypeStruct(layer_out.shape, layer_out.dtype),
+        ],
+        in_specs=[
+            block(gate),
+            pl.BlockSpec((rows, units), lambda i: (jnp.minimum(i, early_steps - 1), 0)),
+            pl.BlockSpec((rows, units), lambda i: (jnp.maximum(i - early_steps, 0), 0)),
+            block(down),
+            block(out),
+            block(query),
+            block(key),
+            block(value),
+            block(tokens_grad),
+            block(layer_out),
+        ],
+        out_specs=[
+            pl.BlockSpec((2, rows, units), lambda i: (0, i, 0)),
+            block(down),
+            block(out),
+            pl.BlockSpec((3, rows, width), lambda i: (0, i, 0)),
+            block(tokens_grad),
+            block(layer_out),
+        ],
+        compiler_params=pltpu.CompilerParams(vmem_limit_bytes=60 << 20),
+        name="widen",
+    )(gate, early_up, late_up, down, out, query, key, value, tokens_grad, layer_out)
+
+
 def banded(line):
     return pltpu.roll(jnp.broadcast_to(line, (WIN, WIN)), 0, 1, stride=1, stride_axis=0)
 
 
-def band_lines(kernel):
-    taps = kernel.shape[2]
-    wide = jnp.pad(kernel, ((0, 0), (0, 0), (0, WIN - taps)))
-    back = jnp.pad(kernel[:, :, ::-1], ((0, 0), (0, 0), (0, WIN - taps)))
-    return jnp.roll(wide, -(taps // 2), axis=2), jnp.roll(back, -(taps // 2), axis=2)
-
-
-def pad_heads(array, axis):
-    shape = array.shape
-    heads = shape[axis] // HEAD_DIM
-    split = array.reshape(shape[:axis] + (heads, HEAD_DIM) + shape[axis + 1 :])
-    widths = [(0, 0)] * split.ndim
-    widths[axis + 1] = (0, PAD_DIM - HEAD_DIM)
-    return jnp.pad(split, widths).reshape(shape[:axis] + (heads * PAD_DIM,) + shape[axis + 1 :])
+def band_line(taps, half, sign):
+    lane = lax.broadcasted_iota(jnp.int32, (1, WIN), 1)
+    line = jnp.zeros((1, WIN), F32)
+    for b in range(taps.shape[1]):
+        line = jnp.where(lane == (sign * (b - half)) % WIN, taps[:, b : b + 1], line)
+    return line
 
 
 def cut_heads(array, axis):
@@ -1323,16 +1437,6 @@
     split = array.reshape(shape[:axis] + (heads, PAD_DIM) + shape[axis + 1 :])
     cut = lax.slice_in_dim(split, 0, HEAD_DIM, axis=axis + 1)
     return cut.reshape(shape[:axis] + (heads * HEAD_DIM,) + shape[axis + 1 :])
-
-
-def windows_needed(start, key_half):
-    length = start.shape[0]
-    first = start[::ROWS]
-    row0 = jnp.arange(0, length, ROWS, dtype=jnp.int32)
-    count = jnp.ones_like(first)
-    for k in range(1, windows_most(key_half)):
-        count = count + (first - key_half < row0 + ROWS - STEP * k).astype(jnp.int32)
-    return count
 
 
 def on_device(
@@ -1345,19 +1449,13 @@
     n_taps, key_taps = kq_kernel.shape[1:]
     key_half = key_taps // 2
 
-    lines, lines_back = band_lines(kq_kernel)
-    gain_heads = pad_heads(group_gain.astype(F32), 0)[None]
-    starts, counts = [], []
-    for n in range(seq_count):
-        seg = segments[n]
-        start = jnp.sum((seg[None, :] < seg[:, None]).astype(jnp.int32), axis=1)
-        counts.append(windows_needed(start, key_half))
-        starts.append(jnp.pad(start, (HALO, 0), constant_values=1 << 20)[:, None])
-
     full_width = w_qkv.shape[1]
-    own_gains = jnp.pad(jnp.stack([attn_gain, mlp_gain]).astype(F32), ((0, 6), (0, 0)))
-    proj, normed_one, scale_one, gains = first_entry(tokens, w_qkv, own_gains)
-    gain_two = gains[1:2]
+    own_gains = jnp.pad(jnp.stack([attn_gain, mlp_gain, group_gain]).astype(F32), ((0, 5), (0, 0)))
+    proj, normed_one, scale_one, gains, gain_heads, start, counts = first_entry(
+        tokens, w_qkv, own_gains, segments, key_half
+    )
+    starts = [start[n * (HALO + length) : (n + 1) * (HALO + length)] for n in range(seq_count)]
+    counts = [counts[n : n + 1] for n in range(seq_count)]
     cot_here, proj = lax.optimization_barrier((cotangent, proj))
     full_cot = lax.all_gather(cot_here, "tensor", axis=1, tiled=True)
 
@@ -1365,12 +1463,12 @@
     for n in range(seq_count):
         rows = slice(n * length, (n + 1) * length)
         kept.append(
-            attend_forward(proj[rows], starts[n], counts[n], lines, head_mix, gain_heads)
+            attend_forward(proj[rows], starts[n], counts[n], kq_kernel, head_mix, gain_heads)
         )
     grouped = jnp.concatenate([one[2] for one in kept], axis=0)
     grouped, full_cot = lax.optimization_barrier((grouped, full_cot))
     hidden_local, hidden, normed_two, w_out_pad, act, grad_gate, grad_up = attn_exit(
-        grouped, w_out, tokens, gain_two, full_cot, w_gate_up, w_down
+        grouped, w_out, tokens, gains, full_cot, w_gate_up, w_down
     )
 
     grad_down = dot_tn(act, full_cot).astype(BF16)
@@ -1379,7 +1477,7 @@
     grad_gate, early_up, grad_down = lax.optimization_barrier((grad_gate, early_up, grad_down))
     early_up, grad_down = lax.psum((early_up, grad_down), "dp")
     grad_attn, grad_hidden_local, grad_gain_two = mlp_exit(
-        grad_gate, grad_up, w_gate_up, hidden, full_cot, hidden_local, cotangent, gain_two,
+        grad_gate, grad_up, w_gate_up, hidden, full_cot, hidden_local, cotangent, gains,
         mlp_gain.astype(F32)[None],
     )
     grad_gate_w = dot_tn(normed_two, grad_gate).astype(BF16)
@@ -1392,7 +1490,7 @@
         rows = slice(n * length, (n + 1) * length)
         parts.append(
             attend_backward(
-                proj[rows], starts[n], counts[n], lines_back, head_mix, gain_heads, kept[n][0], kept[n][1],
+                proj[rows], starts[n], counts[n], kq_kernel, head_mix, gain_heads, kept[n][0], kept[n][1],
                 grad_grouped[rows],
             )
         )
@@ -1413,20 +1511,21 @@
     )
     grad_kernel, grad_mix, grad_group_gain, grad_gain_two = small
     grad_gate_w, late_up, grad_w_out, *grad_qkv = sums
-    grad_gate_up = jnp.stack([grad_gate_w, jnp.concatenate([early_up, late_up], axis=0)])
-    grad_qkv = jnp.stack(grad_qkv)
+    grad_gate_up, grad_down, grad_w_out, grad_qkv, tokens_grad, layer_out = widen(
+        grad_gate_w, early_up, late_up, grad_down, grad_w_out, *grad_qkv, tokens_grad, layer_out
+    )
     return (
         layer_out,
         tokens_grad,
         grad_gain_one,
-        grad_qkv.astype(F32),
+        grad_qkv,
         grad_kernel,
         grad_mix,
         grad_group_gain,
-        grad_w_out.astype(F32),
+        grad_w_out,
         grad_gain_two,
-        grad_gate_up.astype(F32),
-        grad_down.astype(F32),
+        grad_gate_up,
+        grad_down,
     )
 
 

time: 543 us -> 532 us (0.980)
  other arithmetic: 23.7 us -> 2.37 us
  Pallas kernels: 441 us -> 461 us
  local copies, waits for them, and re-layouts: 21.6 us -> 11.7 us
    pallas_call x1 -> x2, Pallas kernels: 24.6 us -> 45.2 us  [the longest x1 28 us: first_entry(): pl.pallas_call(functools.partial(first_entry_kernel, key_half), out_shape...]
    convert_element_type x4 -> x0, other arithmetic: 18.6 us -> none  [the longest x1 5.62 us: on_device(): grad_down.astype(F32)]
    unnamed x54 -> x34, local copies, waits for them, and re-layouts: 11.9 us -> 3.47 us
  transfers between devices with their start and end apart: 2 -> 2, of which waited for: 0 -> 0; matrix products, arithmetic and copies ran while one was open for 9% -> 7% of each run, Pallas kernels for 68% -> 70%
where the time goes in v1:
time: 532 us; the launch traced here: 528 us
  Pallas kernels  461 us (87%)
  matrix products  38.6 us (7%)
  between operations  14.4 us (3%)
  local copies, waits for them, and re-layouts  11.7 us (2%)
    pallas_call x1, Pallas kernels, last_exit(): pl.pallas_call(functools.partial(last_exit_kernel, n_ring, count), out_sh...  206 us
    pallas_call x1, Pallas kernels, attend_backward(): pl.pallas_call(functools.partial(backward_kernel, n_taps, key_half, most)...  68 us
    pallas_call x1, Pallas kernels, mlp_exit(): pl.pallas_call(mlp_exit_kernel, out_shape=[jax.ShapeDtypeStruct((rows, fu...  52.8 us
    pallas_call x1, Pallas kernels, attn_exit(): pl.pallas_call(attn_exit_kernel, out_shape=[jax.ShapeDtypeStruct((rows, w...  47.6 us
    pallas_call x1, Pallas kernels, attend_forward(): pl.pallas_call(functools.partial(forward_kernel, n_taps, key_half, most),...  41.2 us
    dot_general x8, matrix products, dot_tn(): lax.dot_general(a, b, (((0,), (0,)), ((), ())), preferred_element_type=F32)  33.5 us
    pallas_call x1, Pallas kernels, first_entry(): pl.pallas_call(functools.partial(first_entry_kernel, key_half), out_shape...  28 us
    pallas_call x1, Pallas kernels, widen(): pl.pallas_call(functools.partial(widen_kernel, early_steps), grid=(steps,...  17.1 us
  transfers between devices with their start and end apart: 2, of which 0 were waited for; matrix products, arithmetic and copies ran while one was open for 7% of the time, Pallas kernels for 70%

profile of v1, /device:TPU:0, one launch (start us, length us, event | category | flops | bytes accessed | tf_op | source)
XLA Modules:
  0.0 528.4 jit_solution(12052114929024187917)
XLA Ops:
  7.2 0.0 all-gather.2.cloned.1.call-start
  7.2 0.7 stack.14
  7.9 0.7 stack.13
  8.6 0.7 stack.12
  9.3 0.6 fusion.11.gains_ref
  9.9 28.0 %first_entry.1 = (bf16[1024,1536]{1,0:T(8,128)(2,1)}, bf16[1024,1536]{1,0:T(8,128)(2,1)}, f32[1024,1]{1,0:T(8,128)}, f32[8,1536]{1,0:T(8,128)}, f32[1,512]{1,0:T...) custom-call(bf16[1024,384]{1,0:T(8,128)(2,1)} %refs_2_.1, bf16[3,1536,384]{2,1,0:T(8,128)(2,1)} %refs_1_.1, ...), custom_call_target="tpu_custom_call" | custom-call | flops 1048576 | bytes 1024 | tf_op jit(solution)/shard_map/first_entry/pallas_call | solution.py:913
  37.9 0.0 all-gather.2.cloned.1.call-update
  38.0 0.0 all-reduce.7.cloned.1.call-start
  38.0 0.0 copy-done.12
  38.0 0.7 copy.30.mix_ref
  38.7 0.0 copy-done.8
  38.7 0.6 copy.31.base_ref
  39.3 41.2 %attend_forward.1 = (f32[4,8,3,128,256]{4,3,2,1,0:T(8,128)}, f32[1024,512]{1,0:T(8,128)}, bf16[1024,512]{1,0:T(8,128)(2,1)}) custom-call(s32[1,8]{1,0:T(1,128)} %get-tuple-element.59.count_ref, f32[4,2]{1,0:T(4,128)} %copy.30.mix_ref, bf16[1024,1536]{1,0:T(8,128)(2,1)} %get-tuple-element.61.q_ref.k_ref.v_ref, ...), custom_call_target="tpu_custom_call" | custom-call | flops 1048576 | bytes 1024 | tf_op jit(solution)/shard_map/attend_forward/pallas_call | solution.py:191
  80.5 47.6 %attn_exit.1 = (f32[1024,384]{1,0:T(8,128)}, bf16[1024,1536]{1,0:T(8,128)(2,1)}, bf16[1024,1536]{1,0:T(8,128)(2,1)}, bf16[512,1536]{1,0:T(8,128)(2,1)}, bf16[102...) custom-call(bf16[1024,512]{1,0:T(8,128)(2,1)} %get-tuple-element.68.grouped_ref, ...), custom_call_target="tpu_custom_call" | custom-call | flops 1048576 | bytes 1024 | tf_op jit(solution)/shard_map/attn_exit/pallas_call | solution.py:1045
  128.2 0.0 copy-done
  128.2 0.0 copy-start.1
  128.2 6.7 %convolution_convert_fusion.2 = bf16[1024,1536]{1,0:T(8,128)(2,1)} fusion(bf16[1024,1024]{1,0:T(8,128)(2,1)} %get-tuple-element.74.refs_4_, bf16[1024,1536]{1,0:T(8,128)(2,1)S(1)} %copy-done), kind=kOutput, calls=%fused_computation.2 | convolution fusion | flops 3222798336 | bytes 8388608 | tf_op jit(solution)/shard_map/dot_general | solution.py:39
  134.9 4.3 convolution_convert_fusion
  139.2 0.0 all-reduce.7.cloned.1.call-update
  139.2 0.7 copy-done.9
  139.9 0.6 reshape_convert_fusion.gain_local_ref
  140.5 0.0 copy-done.10
  140.5 0.6 reshape_convert_fusion.1.gain_ref
  141.0 52.8 %mlp_exit.1 = (bf16[1024,1536]{1,0:T(8,128)(2,1)}, f32[1024,384]{1,0:T(8,128)}, f32[1,384]{1,0:T(1,128)}) custom-call(bf16[1024,1024]{1,0:T(8,128)(2,1)} %get-tuple-element.75.gate_ref, bf16[1024,1024]{1,0:T(8,128)(2,1)} %get-tuple-element.73.up_ref, bf16[2,1536,1024]{2,1,0:T(8,128)(2,1)} %w_ref.1, bf16[1024,1536]{1,0:T(8,128)(2,1)} %get-tuple-element.76.hidden_in, ...), custom_call_target="tpu_custom_call" | custom-call | flops 1048576 | bytes 1024 | tf_op jit(solution)/shard_map/mlp_exit/pallas_call | solution.py:1137
  193.8 5.1 fusion.12.grad_ref
  198.9 68.0 %attend_backward.1 = (bf16[1024,1152]{1,0:T(8,128)(2,1)}, f32[8,128]{1,0:T(8,128)}, f32[1,512]{1,0:T(1,128)}, f32[4,66,128]{2,1,0:T(8,128)}, f32[2,4,128]{2,1,0:T(4,128)}) custom-call(s32[1,8]{1,0:T(1,128)} %get-tuple-element.59.count_ref, f32[4,2]{1,0:T(4,128)} %copy.30.mix_ref, bf16[1024,1536]{1,0:T(8,128)(2,1)} %get-tuple-element.61.q_ref.k_ref.v_ref, ...), custom_call_target="tpu_custom_call" | custom-call | flops 1048576 | bytes 1024 | tf_op jit(solution)/shard_map/attend_backward/pallas_call | solution.py:402
  267.0 0.8 reshape.96
  267.8 0.8 slice_reduce_fusion.1
  268.5 0.1 reshape_reshape_squeeze.7
  268.6 1.1 slice_reduce_fusion
  269.7 0.1 reshape_reshape_squeeze.6
  269.8 3.9 convolution_convert_fusion.3
  273.7 1.1 slice.68
  274.9 0.6 select_maximum_fusion.small_ref
  275.5 0.2 copy-done.2
  275.7 3.0 convolution_convert_fusion.7
  278.8 4.9 convolution_convert_fusion.6
  283.7 2.9 convolution_convert_fusion.5
  286.6 2.9 convolution_convert_fusion.4
  289.5 4.8 convolution_convert_fusion.1
  294.3 206.3 %last_exit.1 = (f32[1024,384]{1,0:T(8,128)}, bf16[1024,384]{1,0:T(8,128)(2,1)}, f32[16,128]{1,0:T(8,128)}, bf16[8,2,96,1024]{3,2,1,0:T(8,128)(2,1)}, bf16[8,2,24...) custom-call(f32[1024,1]{1,0:T(8,128)} %get-tuple-element.58.factor_r, ...), custom_call_target="tpu_custom_call" | custom-call | flops 1048576 | bytes 1024 | tf_op jit(solution)/shard_map/last_exit/pallas_call | solution.py:1316
  500.7 1.4 slice_bitcast_fusion
  502.0 0.1 reshape.112
  502.1 0.6 copy.32
  502.7 0.7 slice_reduce_fusion.2
  503.4 0.1 reshape.113
  503.5 0.7 copy.33
  504.2 17.1 %widen.1 = (f32[2,1536,1024]{2,1,0:T(8,128)}, f32[1024,1536]{1,0:T(8,128)}, f32[384,1536]{1,0:T(8,128)}, f32[3,1536,384]{2,1,0:T(8,128)}, f32[1024,384]{1,0:T(8,128)}, /*index=5*/bf16[1024,384]{1,0:T(8,128)(2,1)}) custom-call(bf16[1536,1024]{1,0:T(8,128)(2,1)} %bitcast.44, bf16[1152,1024]{1,0:T(8,128)(2,1)} %get-tuple-element.127.early_ref, ...), custom_call_target="tpu_custom_call" | custom-call | tf_op jit(solution)/shard_map/widen/pallas_call | solution.py:1386
  (28 shorter events, 0.1 us)
Async XLA Ops:
  7.2 73.3 %all-gather.2.cloned.1.call-start = ((), (), s32[]{:S(2)}) async-start(), calls=%async_computation | async-start | bytes 3932160 | tf_op jit(solution)/shard_map/all_gather | solution.py:1460
  9.9 28.1 %copy-start.12 = (f32[4,2]{0,1:T(2,128)S(1)}, f32[4,2]{0,1:T(2,128)}, u32[]{:S(2)}) copy-start(f32[4,2]{0,1:T(2,128)} %param.17) | copy-start | bytes 100
  9.9 28.8 %copy-start.8 = (f32[4,6,11]{2,0,1:T(4,128)S(1)}, f32[4,6,11]{2,0,1:T(4,128)}, u32[]{:S(2)}) copy-start(f32[4,6,11]{2,0,1:T(4,128)} %param.16) | copy-start | bytes 3172
  38.0 466.2 %all-reduce.7.cloned.1.call-start = ((), (), s32[]{:S(2)}) async-start(), calls=%async_computation.1 | async-start | bytes 11010048 | tf_op jit(solution)/shard_map/psum | solution.py:1478
  80.5 47.7 %copy-start = (bf16[1024,1536]{1,0:T(8,128)(2,1)S(1)}, bf16[1024,1536]{1,0:T(8,128)(2,1)}, u32[]{:S(2)}) copy-start(bf16[1024,1536]{1,0:T(8,128)(2,1)} %all-gather.2.cloned.1.call-done.cot_in) | copy-start | bytes 9437188
  128.2 6.7 %copy-start.1 = (bf16[1024,1024]{1,0:T(8,128)(2,1)S(1)}, bf16[1024,1024]{1,0:T(8,128)(2,1)}, u32[]{:S(2)}) copy-start(bf16[1024,1024]{1,0:T(8,128)(2,1)} %get-tuple-element.73.up_ref) | copy-start | bytes 6291460
  128.2 6.7 %copy-start.6 = (bf16[1024,1536]{1,0:T(8,128)(2,1)S(1)}, bf16[1024,1536]{1,0:T(8,128)(2,1)}, u32[]{:S(2)}) copy-start(bf16[1024,1536]{1,0:T(8,128)(2,1)} %get-tuple-element.72) | copy-start | bytes 9437188
  139.2 0.7 copy-start.9
  139.2 1.2 copy-start.10
  141.0 52.8 %copy-start.14 = (bf16[512,1536]{1,0:T(8,128)(2,1)S(1)}, bf16[512,1536]{1,0:T(8,128)(2,1)}, u32[]{:S(2)}) copy-start(bf16[512,1536]{1,0:T(8,128)(2,1)} %get-tuple-element.79) | copy-start | bytes 4718596
  198.9 70.9 %copy-start.5 = (bf16[1024,512]{1,0:T(8,128)(2,1)S(1)}, bf16[1024,512]{1,0:T(8,128)(2,1)}, u32[]{:S(2)}) copy-start(bf16[1024,512]{1,0:T(8,128)(2,1)} %get-tuple-element.68.grouped_ref) | copy-start | bytes 3145732
  273.7 1.1 copy-start.11
  273.7 2.0 copy-start.2
  274.9 3.9 copy-start.3
  278.8 4.9 copy-start.13
  286.6 2.9 copy-start.4
  286.6 2.9 copy-start.7
Sparse Core Ops, SparseCore 0:
  38.1 30.1 all-gather.1
  139.4 215.5 all-reduce.6

commit v2 on v1

--- a/solution.py
+++ b/solution.py
@@ -76,7 +76,7 @@
         fill_padded(vs, v_ref, TOP, length)
         for s in range(2):
             for a in range(n_taps):
-                band = banded(band_line(base_ref[s, a : a + 1, :], key_half, 1))
+                band = banded(band_line(base_ref[a, pl.ds(2 * pair + s, 1), :], key_half, 1))
                 high = band.astype(BF16)
                 band_ref[s, a, 0:WIN] = high
                 band_ref[s, a, WIN : 2 * WIN] = high
@@ -140,7 +140,7 @@
                 probs.append(jnp.where(own, prob, 0.0))
             for h in range(2):
                 mixed = (
-                    mix_ref[2 * pair + h, 0] * probs[0] + mix_ref[2 * pair + h, 1] * probs[1]
+                    mix_ref[0, 2 * pair + h] * probs[0] + mix_ref[1, 2 * pair + h] * probs[1]
                 ).astype(BF16)
                 part = dot_nn(mixed, vs[pl.ds(at, WIN), pl.ds(h * PAD_DIM, PAD_DIM)])
                 outs[h] = part if outs[h] is None else outs[h] + part
@@ -157,7 +157,7 @@
 
 def attend_forward(proj, start, counts, base, mix, gain):
     length = proj.shape[0]
-    heads, n_taps = base.shape[:2]
+    n_taps, heads = base.shape[:2]
     pairs = heads // 2
     blocks = length // ROWS
     key_half = 5
@@ -171,7 +171,7 @@
             pl.BlockSpec((length, two), lambda p, b, *_: (0, pairs + p)),
             pl.BlockSpec((length, two), lambda p, b, *_: (0, 2 * pairs + p)),
             pl.BlockSpec((HALO + length, 1), lambda p, b, *_: (0, 0)),
-            pl.BlockSpec((2,) + base.shape[1:], lambda p, b, *_: (p, 0, 0)),
+            pl.BlockSpec(base.shape, lambda p, b, *_: (0, 0, 0)),
             pl.BlockSpec((1, two), lambda p, b, *_: (0, p)),
         ],
         out_specs=[
@@ -226,7 +226,7 @@
         for s in range(2):
             for a in range(n_taps):
                 t_back_ref[s, a * WIN : (a + 1) * WIN, :] = banded(
-                    band_line(base_ref[s, a : a + 1, :], key_half, -1)
+                    band_line(base_ref[a, pl.ds(2 * pair + s, 1), :], key_half, -1)
                 ).astype(BF16)
 
     row0 = pl.multiple_of(block * ROWS, ROWS)
@@ -258,7 +258,7 @@
                     part = jnp.sum(grad_mixed * probs[s], axis=-1, keepdims=True)
                     inner[h][s] = part if inner[h][s] is None else inner[h][s] + part
                 mixed = (
-                    mix_ref[2 * pair + h, 0] * probs[0] + mix_ref[2 * pair + h, 1] * probs[1]
+                    mix_ref[0, 2 * pair + h] * probs[0] + mix_ref[1, 2 * pair + h] * probs[1]
                 ).astype(BF16)
                 dv_sum[pl.ds(at, WIN), cols] += dot_tn(mixed, grads[h])
         for h in range(2):
@@ -271,8 +271,8 @@
         place = row_numbers(row0 - HALO, EXT)
         for s in range(2):
             cols = pl.ds(s * PAD_DIM, PAD_DIM)
-            mix0 = mix_ref[2 * pair, s]
-            mix1 = mix_ref[2 * pair + 1, s]
+            mix0 = mix_ref[s, 2 * pair]
+            mix1 = mix_ref[s, 2 * pair + 1]
             delta = mix0 * inner[0][s] + mix1 * inner[1][s]
             query = qs[pl.ds(row0, EXT), cols]
             for k in range(n):
@@ -355,7 +355,7 @@
 
 def attend_backward(proj, start, counts, base, mix, gain, probs, heads_out, grad_grouped):
     length = proj.shape[0]
-    heads, n_taps = base.shape[:2]
+    n_taps, heads = base.shape[:2]
     pairs = heads // 2
     blocks = length // ROWS
     key_half = 5
@@ -370,7 +370,7 @@
             pl.BlockSpec((length, two), lambda p, b, *_: (0, pairs + p)),
             pl.BlockSpec((length, two), lambda p, b, *_: (0, 2 * pairs + p)),
             pl.BlockSpec((HALO + length, 1), lambda p, b, *_: (0, 0)),
-            pl.BlockSpec((2,) + base.shape[1:], lambda p, b, *_: (p, 0, 0)),
+            pl.BlockSpec(base.shape, lambda p, b, *_: (0, 0, 0)),
             pl.BlockSpec((1, two), lambda p, b, *_: (0, p)),
             pl.BlockSpec((2, 1, most, ROWS, WIN), lambda p, b, *_: (p, b, 0, 0, 0)),
             pl.BlockSpec((ROWS, two), lambda p, b, *_: (b, p)),
@@ -760,8 +760,8 @@
 
 
 def first_entry_kernel(
-    key_half, tokens_ref, w_in, gains_ref, segments_ref, proj_out, normed_out, factor_ref, gains_all_ref, gain_heads_ref,
-    start_ref, count_ref, w_ref, proj_ref, normed_ref, load, store, full, gains_in, send, recv, gains_send, gains_recv,
+    key_half, tokens_ref, w_in, gains_line_ref, segments_ref, proj_out, normed_out, factor_ref, gains_all_ref, gain_heads_ref,
+    start_ref, count_ref, w_ref, proj_ref, normed_ref, load, store, full, gains_ref, gains_in, send, recv, gains_send, gains_recv,
 ):
     weights = pltpu.make_async_copy(w_in, w_ref, load.at[0])
     weights.start()
@@ -802,6 +802,9 @@
             device_id_type=MESH_ID,
         )
 
+    gains_ref[...] = jnp.zeros_like(gains_ref)
+    for n in range(3):
+        gains_ref[n : n + 1, :] = gains_line_ref[:, n * width : (n + 1) * width].astype(F32)
     peers = (near, far, across)
     for kind, peer in enumerate(peers):
         gains_copy(kind, peer, me).start()
@@ -930,6 +933,7 @@
             pltpu.SemaphoreType.DMA((1,)),
             pltpu.SemaphoreType.DMA((2, rows // GROUP)),
             pltpu.VMEM((steps, ranks, CHUNK, width), BF16),
+            pltpu.VMEM((8, width), F32),
             pltpu.VMEM((ranks, 8, width), F32),
             pltpu.SemaphoreType.DMA((3, steps)),
             pltpu.SemaphoreType.DMA((3, steps)),
@@ -1450,7 +1454,8 @@
     key_half = key_taps // 2
 
     full_width = w_qkv.shape[1]
-    own_gains = jnp.pad(jnp.stack([attn_gain, mlp_gain, group_gain]).astype(F32), ((0, 5), (0, 0)))
+    own_gains = jnp.concatenate([attn_gain, mlp_gain, group_gain])[None]
+    taps, mixes = kq_kernel.transpose(1, 0, 2), head_mix.T
     proj, normed_one, scale_one, gains, gain_heads, start, counts = first_entry(
         tokens, w_qkv, own_gains, segments, key_half
     )
@@ -1463,7 +1468,7 @@
     for n in range(seq_count):
         rows = slice(n * length, (n + 1) * length)
         kept.append(
-            attend_forward(proj[rows], starts[n], counts[n], kq_kernel, head_mix, gain_heads)
+            attend_forward(proj[rows], starts[n], counts[n], taps, mixes, gain_heads)
         )
     grouped = jnp.concatenate([one[2] for one in kept], axis=0)
     grouped, full_cot = lax.optimization_barrier((grouped, full_cot))
@@ -1490,7 +1495,7 @@
         rows = slice(n * length, (n + 1) * length)
         parts.append(
             attend_backward(
-                proj[rows], starts[n], counts[n], kq_kernel, head_mix, gain_heads, kept[n][0], kept[n][1],
+                proj[rows], starts[n], counts[n], taps, mixes, gain_heads, kept[n][0], kept[n][1],
                 grad_grouped[rows],
             )
         )

time: 532 us -> 531 us (level)
  no operation moved by 1% of the time
where the time goes in v2:
time: 531 us; the launch traced here: 525 us
  Pallas kernels  460 us (87%)
  matrix products  38.8 us (7%)
  between operations  14.4 us (3%)
  local copies, waits for them, and re-layouts  10.1 us (2%)
    pallas_call x1, Pallas kernels, last_exit(): pl.pallas_call(functools.partial(last_exit_kernel, n_ring, count), out_sh...  210 us
    pallas_call x1, Pallas kernels, attend_backward(): pl.pallas_call(functools.partial(backward_kernel, n_taps, key_half, most)...  66.4 us
    pallas_call x1, Pallas kernels, mlp_exit(): pl.pallas_call(mlp_exit_kernel, out_shape=[jax.ShapeDtypeStruct((rows, fu...  51.7 us
    pallas_call x1, Pallas kernels, attn_exit(): pl.pallas_call(attn_exit_kernel, out_shape=[jax.ShapeDtypeStruct((rows, w...  47.7 us
    pallas_call x1, Pallas kernels, attend_forward(): pl.pallas_call(functools.partial(forward_kernel, n_taps, key_half, most),...  39.3 us
    dot_general x8, matrix products, dot_tn(): lax.dot_general(a, b, (((0,), (0,)), ((), ())), preferred_element_type=F32)  33.8 us
    pallas_call x1, Pallas kernels, first_entry(): pl.pallas_call(functools.partial(first_entry_kernel, key_half), out_shape...  28 us
    pallas_call x1, Pallas kernels, widen(): pl.pallas_call(functools.partial(widen_kernel, early_steps), grid=(steps,...  17.1 us
  transfers between devices with their start and end apart: 2, of which 0 were waited for; matrix products, arithmetic and copies ran while one was open for 7% of the time, Pallas kernels for 70%

profile of v2, /device:TPU:0, one launch (start us, length us, event | category | flops | bytes accessed | tf_op | source)
XLA Modules:
  0.0 525.4 jit_solution(18200371924660222159)
XLA Ops:
  7.2 0.0 all-gather.2.cloned.1.call-start
  7.2 0.7 pad_maximum_fusion
  7.9 0.6 broadcast_in_dim.13.gains_line_ref
  8.5 28.0 %first_entry.1 = (bf16[1024,1536]{1,0:T(8,128)(2,1)}, bf16[1024,1536]{1,0:T(8,128)(2,1)}, f32[1024,1]{1,0:T(8,128)}, f32[8,1536]{1,0:T(8,128)}, f32[1,512]{1,0:T...) custom-call(bf16[1024,384]{1,0:T(8,128)(2,1)} %refs_2_.1, bf16[3,1536,384]{2,1,0:T(8,128)(2,1)} %refs_1_.1, ...), custom_call_target="tpu_custom_call" | custom-call | flops 1048576 | bytes 1024 | tf_op jit(solution)/shard_map/first_entry/pallas_call | solution.py:916
  36.6 0.0 all-gather.2.cloned.1.call-update
  36.6 0.2 all-reduce.6.cloned.1.call-start
  36.8 39.3 %attend_forward.1 = (f32[4,8,3,128,256]{4,3,2,1,0:T(8,128)}, f32[1024,512]{1,0:T(8,128)}, bf16[1024,512]{1,0:T(8,128)(2,1)}) custom-call(s32[1,8]{1,0:T(1,128)} %get-tuple-element.59.count_ref, f32[2,4]{1,0:T(2,128)} %bitcast.61, bf16[1024,1536]{1,0:T(8,128)(2,1)} %get-tuple-element.61.q_ref.k_ref.v_ref, ...), custom_call_target="tpu_custom_call" | custom-call | flops 1048576 | bytes 1024 | tf_op jit(solution)/shard_map/attend_forward/pallas_call | solution.py:191
  76.1 0.0 copy-start
  76.1 47.7 %attn_exit.1 = (f32[1024,384]{1,0:T(8,128)}, bf16[1024,1536]{1,0:T(8,128)(2,1)}, bf16[1024,1536]{1,0:T(8,128)(2,1)}, bf16[512,1536]{1,0:T(8,128)(2,1)}, bf16[102...) custom-call(bf16[1024,512]{1,0:T(8,128)(2,1)} %get-tuple-element.68.grouped_ref, ...), custom_call_target="tpu_custom_call" | custom-call | flops 1048576 | bytes 1024 | tf_op jit(solution)/shard_map/attn_exit/pallas_call | solution.py:1049
  123.8 0.0 copy-done
  123.8 0.0 copy-start.1
  123.8 0.0 copy-start.6
  123.8 6.7 %convolution_convert_fusion.2 = bf16[1024,1536]{1,0:T(8,128)(2,1)} fusion(bf16[1024,1024]{1,0:T(8,128)(2,1)} %get-tuple-element.74.refs_4_, bf16[1024,1536]{1,0:T(8,128)(2,1)S(1)} %copy-done), kind=kOutput, calls=%fused_computation.2 | convolution fusion | flops 3222798336 | bytes 8388608 | tf_op jit(solution)/shard_map/dot_general | solution.py:39
  130.5 4.3 convolution_convert_fusion
  134.8 0.0 all-reduce.6.cloned.1.call-update
  134.9 0.7 copy-done.8
  135.5 0.6 reshape.116.gain_local_ref
  136.1 0.0 copy-done.9
  136.1 0.6 reshape.117.gain_ref
  136.7 51.7 %mlp_exit.1 = (bf16[1024,1536]{1,0:T(8,128)(2,1)}, f32[1024,384]{1,0:T(8,128)}, f32[1,384]{1,0:T(1,128)}) custom-call(bf16[1024,1024]{1,0:T(8,128)(2,1)} %get-tuple-element.75.gate_ref, bf16[1024,1024]{1,0:T(8,128)(2,1)} %get-tuple-element.73.up_ref, bf16[2,1536,1024]{2,1,0:T(8,128)(2,1)} %w_ref.1, bf16[1024,1536]{1,0:T(8,128)(2,1)} %get-tuple-element.76.hidden_in, ...), custom_call_target="tpu_custom_call" | custom-call | flops 1048576 | bytes 1024 | tf_op jit(solution)/shard_map/mlp_exit/pallas_call | solution.py:1141
  188.4 5.0 fusion.6.grad_ref
  193.4 66.4 %attend_backward.1 = (bf16[1024,1152]{1,0:T(8,128)(2,1)}, f32[8,128]{1,0:T(8,128)}, f32[1,512]{1,0:T(1,128)}, f32[4,66,128]{2,1,0:T(8,128)}, f32[2,4,128]{2,1,0:T(4,128)}) custom-call(s32[1,8]{1,0:T(1,128)} %get-tuple-element.59.count_ref, f32[2,4]{1,0:T(2,128)} %bitcast.62, bf16[1024,1536]{1,0:T(8,128)(2,1)} %get-tuple-element.61.q_ref.k_ref.v_ref, ...), custom_call_target="tpu_custom_call" | custom-call | flops 1048576 | bytes 1024 | tf_op jit(solution)/shard_map/attend_backward/pallas_call | solution.py:402
  259.8 0.8 reshape.96
  260.5 0.8 slice_reduce_fusion.1
  261.3 0.1 reshape_reshape_squeeze.7
  261.4 1.1 slice_reduce_fusion
  262.4 0.1 reshape_reshape_squeeze.6
  262.5 4.2 convolution_convert_fusion.3
  266.8 0.0 copy-start.10
  266.8 0.0 copy-start.2
  266.8 1.1 slice.68
  267.9 0.0 copy-done.10
  267.9 0.6 select_maximum_fusion.small_ref
  268.6 0.3 copy-done.2
  268.9 3.0 convolution_convert_fusion.7
  271.9 4.9 convolution_convert_fusion.6
  276.8 0.0 copy-done.11
  276.8 2.9 convolution_convert_fusion.5
  279.7 2.9 convolution_convert_fusion.4
  282.6 4.9 convolution_convert_fusion.1
  287.5 210.2 %last_exit.1 = (f32[1024,384]{1,0:T(8,128)}, bf16[1024,384]{1,0:T(8,128)(2,1)}, f32[16,128]{1,0:T(8,128)}, bf16[8,2,96,1024]{3,2,1,0:T(8,128)(2,1)}, bf16[8,2,24...) custom-call(f32[1024,1]{1,0:T(8,128)} %get-tuple-element.58.factor_r, ...), custom_call_target="tpu_custom_call" | custom-call | flops 1048576 | bytes 1024 | tf_op jit(solution)/shard_map/last_exit/pallas_call | solution.py:1320
  497.6 1.4 slice_bitcast_fusion
  499.0 0.1 reshape.112
  499.1 0.6 copy.24
  499.7 0.7 slice_reduce_fusion.2
  500.4 0.1 reshape.113
  500.5 0.7 copy.25
  501.1 17.1 %widen.1 = (f32[2,1536,1024]{2,1,0:T(8,128)}, f32[1024,1536]{1,0:T(8,128)}, f32[384,1536]{1,0:T(8,128)}, f32[3,1536,384]{2,1,0:T(8,128)}, f32[1024,384]{1,0:T(8,128)}, /*index=5*/bf16[1024,384]{1,0:T(8,128)(2,1)}) custom-call(bf16[1536,1024]{1,0:T(8,128)(2,1)} %bitcast.46, bf16[1152,1024]{1,0:T(8,128)(2,1)} %get-tuple-element.127.early_ref, ...), custom_call_target="tpu_custom_call" | custom-call | tf_op jit(solution)/shard_map/widen/pallas_call | solution.py:1390
  (20 shorter events, 0.1 us)
Async XLA Ops:
  7.2 68.9 %all-gather.2.cloned.1.call-start = ((), (), s32[]{:S(2)}) async-start(), calls=%async_computation | async-start | bytes 3932160 | tf_op jit(solution)/shard_map/all_gather | solution.py:1465
  36.6 464.5 %all-reduce.6.cloned.1.call-start = ((), (), s32[]{:S(2)}) async-start(), calls=%async_computation.1 | async-start | bytes 11010048 | tf_op jit(solution)/shard_map/psum | solution.py:1483
  76.1 47.7 %copy-start = (bf16[1024,1536]{1,0:T(8,128)(2,1)S(1)}, bf16[1024,1536]{1,0:T(8,128)(2,1)}, u32[]{:S(2)}) copy-start(bf16[1024,1536]{1,0:T(8,128)(2,1)} %all-gather.2.cloned.1.call-done.cot_in) | copy-start | bytes 9437188
  123.8 6.7 %copy-start.1 = (bf16[1024,1024]{1,0:T(8,128)(2,1)S(1)}, bf16[1024,1024]{1,0:T(8,128)(2,1)}, u32[]{:S(2)}) copy-start(bf16[1024,1024]{1,0:T(8,128)(2,1)} %get-tuple-element.73.up_ref) | copy-start | bytes 6291460
  123.8 6.7 %copy-start.6 = (bf16[1024,1536]{1,0:T(8,128)(2,1)S(1)}, bf16[1024,1536]{1,0:T(8,128)(2,1)}, u32[]{:S(2)}) copy-start(bf16[1024,1536]{1,0:T(8,128)(2,1)} %get-tuple-element.72) | copy-start | bytes 9437188
  134.8 0.7 copy-start.8
  134.8 1.2 copy-start.9
  136.7 51.7 %copy-start.12 = (bf16[512,1536]{1,0:T(8,128)(2,1)S(1)}, bf16[512,1536]{1,0:T(8,128)(2,1)}, u32[]{:S(2)}) copy-start(bf16[512,1536]{1,0:T(8,128)(2,1)} %get-tuple-element.79) | copy-start | bytes 4718596
  193.4 69.1 %copy-start.5 = (bf16[1024,512]{1,0:T(8,128)(2,1)S(1)}, bf16[1024,512]{1,0:T(8,128)(2,1)}, u32[]{:S(2)}) copy-start(bf16[1024,512]{1,0:T(8,128)(2,1)} %get-tuple-element.68.grouped_ref) | copy-start | bytes 3145732
  266.8 1.1 copy-start.10
  266.8 2.1 copy-start.2
  267.9 4.0 copy-start.3
  271.9 4.9 copy-start.11
  279.7 2.9 copy-start.4
  279.7 2.9 copy-start.7
Sparse Core Ops, SparseCore 0:
  36.7 30.1 all-gather.1
  135.0 216.7 all-reduce.5

commit v3 on v2

--- a/solution.py
+++ b/solution.py
@@ -445,7 +445,7 @@
     return array.reshape(n, 2, -1, array.shape[-1])
 
 
-def make_ring(n, sources, ins, outs, scratch):
+def make_ring(n, sources, ins, outs, finals, leave_sem, scratch):
     count = len(ins)
     slots = scratch[:count]
     rs_send, rs_recv, ag_send, ag_recv = scratch[count:]
@@ -480,6 +480,9 @@
 
     both = [(k, way) for k in range(count) for way in range(2)]
 
+    def leave(way, k, c):
+        return pltpu.make_async_copy(outs[k].at[c, way], finals[k].at[c, way], leave_sem.at[way, k, c])
+
     def start():
         for k, way in both:
             sum_copy(way, k, 0, sources[k].at[chunk(way, 1), way]).start()
@@ -498,6 +501,7 @@
                 sum_copy(way, k, n - 2, slots[k].at[way, n - 2]).wait_recv()
                 add(way, k, n - 2, place, outs[k].at[place, way])
                 share_copy(way, k, 0, place).start()
+                leave(way, k, place).start()
 
         @pl.when((now > n - 2) & (now < 2 * n - 3))
         def _():
@@ -505,11 +509,13 @@
             for k, way in both:
                 share_copy(way, k, step, chunk(way, step + 1)).wait_recv()
                 share_copy(way, k, step + 1, chunk(way, step + 1)).start()
+                leave(way, k, chunk(way, step + 1)).start()
 
         @pl.when(now == 2 * n - 3)
         def _():
             for k, way in both:
                 share_copy(way, k, n - 2, chunk(way, n - 1)).wait_recv()
+                leave(way, k, chunk(way, n - 1)).start()
 
     def drain():
         def one(s, carry):
@@ -519,6 +525,13 @@
             return carry
 
         lax.fori_loop(0, n - 1, one, 0)
+
+        def left(c, carry):
+            for k, way in both:
+                leave(way, k, c).wait()
+            return carry
+
+        lax.fori_loop(0, n, left, 0)
 
     return start, tick, drain
 
@@ -1167,8 +1180,9 @@
 ):
     given, sources, refs = refs[:7], refs[7 : 7 + count], refs[7 + count :]
     tokens_grad_ref, out_ref, small_sum_ref = refs[:3]
-    outs, refs = refs[3 : 3 + count], refs[3 + count :]
+    finals, refs = refs[3 : 3 + count], refs[3 + count :]
     here_too, ins, load, refs = refs[:7], refs[7 : 7 + count], refs[7 + count], refs[8 + count :]
+    outs, leave_sem, refs = refs[:count], refs[count], refs[count + 1 :]
     grad_ref, w_ref, tokens_ref, grad_hidden_ref, act_ref, w_down_ref, hidden_ref = here_too
     loads = [
         pltpu.make_async_copy(src, dst, load.at[n])
@@ -1282,7 +1296,7 @@
     lax.fori_loop(1, n_ring, greet, 0)
     pl.semaphore_wait(barrier, 2 + n_ring - 1)
 
-    ring_start, ring_tick, ring_drain = make_ring(n_ring, sources, ins, outs, ring_refs)
+    ring_start, ring_tick, ring_drain = make_ring(n_ring, sources, ins, outs, finals, leave_sem, ring_refs)
     tick, ticks, drain = make_exchange(2 * half, scratch, partial, local, between, GROUP)
     ring_start()
     for one in loads:
@@ -1326,10 +1340,14 @@
         ]
         + [jax.ShapeDtypeStruct(a.shape, a.dtype) for a in split],
         in_specs=[vmem] * 4 + [pl.BlockSpec(memory_space=pl.ANY)] * (7 + count),
-        out_specs=[vmem] * (3 + count),
+        out_specs=[vmem] * 3 + [pl.BlockSpec(memory_space=pl.ANY)] * count,
         scratch_shapes=[pltpu.VMEM(a.shape, a.dtype) for a in (*given, *split)]
         + [
             pltpu.SemaphoreType.DMA((7 + count,)),
+        ]
+        + [pltpu.VMEM(a.shape, a.dtype) for a in split]
+        + [
+            pltpu.SemaphoreType.DMA((2, count, n_ring)),
             pltpu.VMEM((1, width), F32),
             pltpu.VMEM(packed.shape, F32),
             pltpu.VMEM((n_ring,) + packed.shape, F32),

time: 531 us -> 531 us (level)
  no operation moved by 1% of the time
where the time goes in v3:
time: 531 us; the launch traced here: 525 us
  Pallas kernels  461 us (87%)
  matrix products  38.8 us (7%)
  between operations  14.4 us (3%)
  local copies, waits for them, and re-layouts  10 us (2%)
    pallas_call x1, Pallas kernels, last_exit(): pl.pallas_call(functools.partial(last_exit_kernel, n_ring, count), out_sh...  215 us
    pallas_call x1, Pallas kernels, attend_backward(): pl.pallas_call(functools.partial(backward_kernel, n_taps, key_half, most)...  64.1 us
    pallas_call x1, Pallas kernels, mlp_exit(): pl.pallas_call(mlp_exit_kernel, out_shape=[jax.ShapeDtypeStruct((rows, fu...  51.5 us
    pallas_call x1, Pallas kernels, attn_exit(): pl.pallas_call(attn_exit_kernel, out_shape=[jax.ShapeDtypeStruct((rows, w...  47.6 us
    pallas_call x1, Pallas kernels, attend_forward(): pl.pallas_call(functools.partial(forward_kernel, n_taps, key_half, most),...  37.5 us
    dot_general x8, matrix products, dot_tn(): lax.dot_general(a, b, (((0,), (0,)), ((), ())), preferred_element_type=F32)  33.7 us
    pallas_call x1, Pallas kernels, first_entry(): pl.pallas_call(functools.partial(first_entry_kernel, key_half), out_shape...  28 us
    pallas_call x1, Pallas kernels, widen(): pl.pallas_call(functools.partial(widen_kernel, early_steps), grid=(steps,...  17.1 us
  transfers between devices with their start and end apart: 2, of which 0 were waited for; matrix products, arithmetic and copies ran while one was open for 7% of the time, Pallas kernels for 70%

profile of v3, /device:TPU:0, one launch (start us, length us, event | category | flops | bytes accessed | tf_op | source)
XLA Modules:
  0.0 525.5 jit_solution(12316491842723950007)
XLA Ops:
  7.2 0.0 all-gather.2.cloned.1.call-start
  7.2 0.7 pad_maximum_fusion
  7.9 0.6 broadcast_in_dim.13.gains_line_ref
  8.5 28.0 %first_entry.1 = (bf16[1024,1536]{1,0:T(8,128)(2,1)}, bf16[1024,1536]{1,0:T(8,128)(2,1)}, f32[1024,1]{1,0:T(8,128)}, f32[8,1536]{1,0:T(8,128)}, f32[1,512]{1,0:T...) custom-call(bf16[1024,384]{1,0:T(8,128)(2,1)} %refs_2_.1, bf16[3,1536,384]{2,1,0:T(8,128)(2,1)} %refs_1_.1, ...), custom_call_target="tpu_custom_call" | custom-call | flops 1048576 | bytes 1024 | tf_op jit(solution)/shard_map/first_entry/pallas_call | solution.py:929
  36.6 0.0 all-gather.2.cloned.1.call-update
  36.6 0.2 all-reduce.6.cloned.1.call-start
  36.8 37.5 %attend_forward.1 = (f32[4,8,3,128,256]{4,3,2,1,0:T(8,128)}, f32[1024,512]{1,0:T(8,128)}, bf16[1024,512]{1,0:T(8,128)(2,1)}) custom-call(s32[1,8]{1,0:T(1,128)} %get-tuple-element.59.count_ref, f32[2,4]{1,0:T(2,128)} %bitcast.61, bf16[1024,1536]{1,0:T(8,128)(2,1)} %get-tuple-element.61.q_ref.k_ref.v_ref, ...), custom_call_target="tpu_custom_call" | custom-call | flops 1048576 | bytes 1024 | tf_op jit(solution)/shard_map/attend_forward/pallas_call | solution.py:191
  74.4 0.0 copy-start
  74.4 47.6 %attn_exit.1 = (f32[1024,384]{1,0:T(8,128)}, bf16[1024,1536]{1,0:T(8,128)(2,1)}, bf16[1024,1536]{1,0:T(8,128)(2,1)}, bf16[512,1536]{1,0:T(8,128)(2,1)}, bf16[102...) custom-call(bf16[1024,512]{1,0:T(8,128)(2,1)} %get-tuple-element.68.grouped_ref, ...), custom_call_target="tpu_custom_call" | custom-call | flops 1048576 | bytes 1024 | tf_op jit(solution)/shard_map/attn_exit/pallas_call | solution.py:1062
  122.0 0.0 copy-done
  122.0 0.0 copy-start.1
  122.0 0.0 copy-start.6
  122.1 6.7 %convolution_convert_fusion.2 = bf16[1024,1536]{1,0:T(8,128)(2,1)} fusion(bf16[1024,1024]{1,0:T(8,128)(2,1)} %get-tuple-element.74.refs_4_, bf16[1024,1536]{1,0:T(8,128)(2,1)S(1)} %copy-done), kind=kOutput, calls=%fused_computation.2 | convolution fusion | flops 3222798336 | bytes 8388608 | tf_op jit(solution)/shard_map/dot_general | solution.py:39
  128.7 0.0 copy-done.1
  128.7 0.0 copy-done.6
  128.7 4.3 convolution_convert_fusion
  133.1 0.0 all-reduce.6.cloned.1.call-update
  133.1 0.7 copy-done.8
  133.7 0.6 reshape.116.gain_local_ref
  134.3 0.0 copy-done.9
  134.3 0.6 reshape.117.gain_ref
  134.9 51.5 %mlp_exit.1 = (bf16[1024,1536]{1,0:T(8,128)(2,1)}, f32[1024,384]{1,0:T(8,128)}, f32[1,384]{1,0:T(1,128)}) custom-call(bf16[1024,1024]{1,0:T(8,128)(2,1)} %get-tuple-element.75.gate_ref, bf16[1024,1024]{1,0:T(8,128)(2,1)} %get-tuple-element.73.up_ref, bf16[2,1536,1024]{2,1,0:T(8,128)(2,1)} %w_ref.1, bf16[1024,1536]{1,0:T(8,128)(2,1)} %get-tuple-element.76.hidden_in, ...), custom_call_target="tpu_custom_call" | custom-call | flops 1048576 | bytes 1024 | tf_op jit(solution)/shard_map/mlp_exit/pallas_call | solution.py:1154
  186.4 0.0 copy-done.12
  186.4 5.0 fusion.6.grad_ref
  191.5 64.1 %attend_backward.1 = (bf16[1024,1152]{1,0:T(8,128)(2,1)}, f32[8,128]{1,0:T(8,128)}, f32[1,512]{1,0:T(1,128)}, f32[4,66,128]{2,1,0:T(8,128)}, f32[2,4,128]{2,1,0:T(4,128)}) custom-call(s32[1,8]{1,0:T(1,128)} %get-tuple-element.59.count_ref, f32[2,4]{1,0:T(2,128)} %bitcast.62, bf16[1024,1536]{1,0:T(8,128)(2,1)} %get-tuple-element.61.q_ref.k_ref.v_ref, ...), custom_call_target="tpu_custom_call" | custom-call | flops 1048576 | bytes 1024 | tf_op jit(solution)/shard_map/attend_backward/pallas_call | solution.py:402
  255.5 0.8 reshape.96
  256.3 0.8 slice_reduce_fusion.1
  257.1 0.1 reshape_reshape_squeeze.7
  257.2 1.1 slice_reduce_fusion
  258.2 0.1 reshape_reshape_squeeze.6
  258.3 3.7 convolution_convert_fusion.3
  262.1 1.1 slice.68
  263.2 0.6 select_maximum_fusion.small_ref
  263.9 0.2 copy-done.2
  264.1 3.1 convolution_convert_fusion.7
  267.2 5.3 %convolution_convert_fusion.6 = bf16[1536,384]{1,0:T(8,128)(2,1)} fusion(bf16[1024,1536]{1,0:T(8,128)(2,1)} %get-tuple-element.87, bf16[1024,1152]{1,0:T(8,128)(2,1)S(1)} %copy-done.3), kind=kOutput, calls=%fused_computation.6 | convolution fusion | flops 1208549376 | bytes 5111808 | tf_op jit(solution)/shard_map/dot_general | solution.py:39
  272.5 2.9 convolution_convert_fusion.5
  275.4 2.9 convolution_convert_fusion.4
  278.2 0.0 copy-done.7
  278.2 4.8 convolution_convert_fusion.1
  283.1 214.7 %last_exit.1 = (f32[1024,384]{1,0:T(8,128)}, bf16[1024,384]{1,0:T(8,128)(2,1)}, f32[16,128]{1,0:T(8,128)}, bf16[8,2,96,1024]{3,2,1,0:T(8,128)(2,1)}, bf16[8,2,24...) custom-call(f32[1024,1]{1,0:T(8,128)} %get-tuple-element.58.factor_r, ...), custom_call_target="tpu_custom_call" | custom-call | flops 1048576 | bytes 1024 | tf_op jit(solution)/shard_map/last_exit/pallas_call | solution.py:1334
  497.8 1.4 slice_bitcast_fusion
  499.1 0.1 reshape.112
  499.2 0.6 copy.24
  499.8 0.7 slice_reduce_fusion.2
  500.5 0.1 reshape.113
  500.6 0.7 copy.25
  501.3 17.1 %widen.1 = (f32[2,1536,1024]{2,1,0:T(8,128)}, f32[1024,1536]{1,0:T(8,128)}, f32[384,1536]{1,0:T(8,128)}, f32[3,1536,384]{2,1,0:T(8,128)}, f32[1024,384]{1,0:T(8,128)}, /*index=5*/bf16[1024,384]{1,0:T(8,128)(2,1)}) custom-call(bf16[1536,1024]{1,0:T(8,128)(2,1)} %bitcast.46, bf16[1152,1024]{1,0:T(8,128)(2,1)} %get-tuple-element.127.early_ref, ...), custom_call_target="tpu_custom_call" | custom-call | tf_op jit(solution)/shard_map/widen/pallas_call | solution.py:1408
  (20 shorter events, 0.1 us)
Async XLA Ops:
  7.2 67.2 %all-gather.2.cloned.1.call-start = ((), (), s32[]{:S(2)}) async-start(), calls=%async_computation | async-start | bytes 3932160 | tf_op jit(solution)/shard_map/all_gather | solution.py:1483
  36.6 464.7 %all-reduce.6.cloned.1.call-start = ((), (), s32[]{:S(2)}) async-start(), calls=%async_computation.1 | async-start | bytes 11010048 | tf_op jit(solution)/shard_map/psum | solution.py:1501
  74.4 47.7 %copy-start = (bf16[1024,1536]{1,0:T(8,128)(2,1)S(1)}, bf16[1024,1536]{1,0:T(8,128)(2,1)}, u32[]{:S(2)}) copy-start(bf16[1024,1536]{1,0:T(8,128)(2,1)} %all-gather.2.cloned.1.call-done.cot_in) | copy-start | bytes 9437188
  122.0 6.7 %copy-start.1 = (bf16[1024,1024]{1,0:T(8,128)(2,1)S(1)}, bf16[1024,1024]{1,0:T(8,128)(2,1)}, u32[]{:S(2)}) copy-start(bf16[1024,1024]{1,0:T(8,128)(2,1)} %get-tuple-element.73.up_ref) | copy-start | bytes 6291460
  122.0 6.7 %copy-start.6 = (bf16[1024,1536]{1,0:T(8,128)(2,1)S(1)}, bf16[1024,1536]{1,0:T(8,128)(2,1)}, u32[]{:S(2)}) copy-start(bf16[1024,1536]{1,0:T(8,128)(2,1)} %get-tuple-element.72) | copy-start | bytes 9437188
  133.1 0.7 copy-start.8
  133.1 1.2 copy-start.9
  134.9 51.5 %copy-start.12 = (bf16[512,1536]{1,0:T(8,128)(2,1)S(1)}, bf16[512,1536]{1,0:T(8,128)(2,1)}, u32[]{:S(2)}) copy-start(bf16[512,1536]{1,0:T(8,128)(2,1)} %get-tuple-element.79) | copy-start | bytes 4718596
  191.5 66.8 %copy-start.5 = (bf16[1024,512]{1,0:T(8,128)(2,1)S(1)}, bf16[1024,512]{1,0:T(8,128)(2,1)}, u32[]{:S(2)}) copy-start(bf16[1024,512]{1,0:T(8,128)(2,1)} %get-tuple-element.68.grouped_ref) | copy-start | bytes 3145732
  262.1 1.1 copy-start.10
  262.1 2.0 copy-start.2
  263.2 4.0 copy-start.3
  267.2 5.3 %copy-start.11 = (bf16[1024,1536]{1,0:T(8,128)(2,1)S(1)}, bf16[1024,1536]{1,0:T(8,128)(2,1)}, u32[]{:S(2)}) copy-start(bf16[1024,1536]{1,0:T(8,128)(2,1)} %get-tuple-element.87) | copy-start | bytes 9437188
  275.4 2.9 copy-start.4
  275.4 2.9 copy-start.7
Sparse Core Ops, SparseCore 0:
  36.7 30.1 all-gather.1
  133.2 220.7 all-reduce.5
